TPU v7x, 256 devices: a whole 4x4x8 slice. The times are simulated.
256 devices in a mesh: blk: 128 (over y, z, x_lo, core), rhs: 2 (over x_hi).
Axes of the slice: x: 4 (x_hi: 2, x_lo: 2; x = x_hi * 2 + x_lo), y: 4, z: 8, core: 2. Of those that a mesh axis runs over, the one named last changes fastest.
Arguments:
- positions: float32 [3, 32768], P(None, 'blk'), may hold values from -1 to 1
- normal_angles: float32 [2, 32768], P(None, 'blk'), may hold values from -3.140625 to 3.140625
- areas: float32 [32768], P('blk'), may hold values from 1 to 6
- densities: float32 [2, 2, 32768], P('rhs', None, 'blk'), may hold values from -6 to 6
- need_owner: int32 [32768, 1], P('blk'), may hold values from 0 to 127; in each aligned block of 256 rows (0 to 255, 256 to 511, ...) at most 8 rows name the same one
- need_slot: int32 [32768], P('blk'), may hold values from 0 to 255
- near_index: int32 [32, 32768], P(None, 'blk'), may hold values from 0 to 255
- near_coef: float32 [2, 32, 32768], P(None, None, 'blk'), may hold values from -2 to 2
Outputs:
- result_field: float32 [2, 2, 32768], P('rhs', None, 'blk')
Inputs may be any that keep to these rules, and one draw needn't show every extreme that they name: `need_owner`: among the 256 entries of one block of targets, at most 8 name the same owner.
All inputs are finite; a program needn't handle non-finite values.
Results may differ from a plain program's by a relative error of at most 0.0003.
Values sent between devices are 32-bit elements; how exact they have to be, the bound alone decides.
A program may use at most 128 MiB of HBM per device.

v0:
```python
import math

import jax
import jax.numpy as jnp
from jax import lax
from jax.sharding import PartitionSpec as P

WAVE = 8.0
COUPLE = 1.0
SOFT = 0.1
TILE = 512


def unit_normals(angles):
    azimuth = angles[0]
    elevation = angles[1]
    return jnp.stack(
        [
            jnp.cos(azimuth) * jnp.cos(elevation),
            jnp.sin(azimuth) * jnp.cos(elevation),
            jnp.sin(elevation),
        ],
        0,
    )


def kernel_tile(targets, geometry):
    offset_vec = targets[:, :, None] - geometry[0:3, None, :]
    distance = jnp.sqrt(jnp.sum(offset_vec * offset_vec, 0) + SOFT * SOFT)
    facing = jnp.sum(offset_vec * geometry[3:6, None, :], 0)
    single = 1.0 / (4.0 * math.pi * distance)
    double = facing * single / (distance * distance)
    phases = WAVE * distance
    cosine = jnp.cos(phases)
    sines = jnp.sin(phases)
    weight = geometry[6][None, :]
    real_part = weight * (double * (cosine + phases * sines) + COUPLE * single * sines)
    imag_part = weight * (double * (sines - phases * cosine) - COUPLE * single * cosine)
    return (real_part, imag_part)


def apply_tile(targets, geometry, sources):
    real_part, imag_part = kernel_tile(targets, geometry)
    highest = lax.Precision.HIGHEST
    src_real = sources[:, 0, :]
    src_imag = sources[:, 1, :]
    out_real = jnp.einsum("ts,rs->rt", real_part, src_real, precision=highest) - jnp.einsum(
        "ts,rs->rt", imag_part, src_imag, precision=highest
    )
    out_imag = jnp.einsum("ts,rs->rt", real_part, src_imag, precision=highest) + jnp.einsum(
        "ts,rs->rt", imag_part, src_real, precision=highest
    )
    return (out_real, out_imag)


def far_block(running, targets, geometry, sources):
    more_real, more_imag = apply_tile(targets, geometry, sources)
    return (running[0] + more_real, running[1] + more_imag)


def far_piece(running, targets, geometry, flat_sources):
    count_rows = geometry.shape[1]
    side_count = flat_sources.shape[0] // 2
    sources = flat_sources.reshape(side_count, 2, count_rows)
    tile_width = math.gcd(count_rows, TILE)
    blocks = count_rows // tile_width
    geo_tiles = geometry.reshape(7, blocks, tile_width).transpose(1, 0, 2)
    src_tiles = sources.reshape(side_count, 2, blocks, tile_width).transpose(2, 0, 1, 3)

    def advance(partial_sums, tile_pair):
        return (far_block(partial_sums, targets, tile_pair[0], tile_pair[1]), None)

    running, _ = lax.scan(advance, running, (geo_tiles, src_tiles))
    return running


def near_field(needed, near_rows, near_terms):
    looked = needed[:, :, near_rows]
    coef_real = near_terms[0]
    coef_imag = near_terms[1]
    near_real = jnp.sum(coef_real * looked[:, 0] - coef_imag * looked[:, 1], 1)
    near_imag = jnp.sum(coef_real * looked[:, 1] + coef_imag * looked[:, 0], 1)
    return (near_real, near_imag)


def on_device(
    positions, normal_angles, areas, densities, need_owner, need_slot, near_index, near_coef
):
    own_rows = positions.shape[1]
    blk_count = lax.axis_size("blk")
    panels_all = own_rows * blk_count
    normals = unit_normals(normal_angles)
    weights = areas * (1.0 / math.sqrt(panels_all))
    geometry = jnp.concatenate([positions, normals, weights[None, :]], 0)
    owners = need_owner[:, 0]
    need_count = need_slot.shape[0]
    send_density = densities.reshape(2 * densities.shape[0], own_rows)
    side_count = send_density.shape[0] // 2
    target_count = positions.shape[1]
    empty_sum = jnp.zeros((side_count, target_count), jnp.float32)
    far_real, far_imag = far_piece(
        (empty_sum, empty_sum),
        positions,
        lax.all_gather(geometry, "blk", axis=1, tiled=True),
        lax.all_gather(send_density, "blk", axis=1, tiled=True),
    )
    near_sides = densities.shape[0]
    capacity = 4 * need_count // blk_count
    owner_ids = jnp.arange(blk_count, dtype=jnp.int32)
    onehot = (owners[:, None] == owner_ids[None, :]).astype(jnp.int32)
    before = jnp.cumsum(onehot, 0) - onehot
    ranks_in = jnp.sum(before * onehot, 1)
    placed = owners * capacity + ranks_in
    requests = (
        jnp.zeros((blk_count * capacity,), jnp.int32)
        .at[placed]
        .set(need_slot)
        .reshape(blk_count, capacity)
    )
    values = densities[
        :, :, lax.all_to_all(requests, "blk", split_axis=0, concat_axis=0, tiled=True)
    ]
    answers = lax.all_to_all(values, "blk", split_axis=2, concat_axis=2, tiled=True)
    needed = answers.reshape(near_sides, 2, blk_count * capacity)[:, :, placed]
    near_real, near_imag = near_field(needed, near_index, near_coef)
    far_real = far_real + near_real
    far_imag = far_imag + near_imag
    field_real = 0.5 * densities[:, 0] + far_real
    field_imag = 0.5 * densities[:, 1] + far_imag
    result_field = jnp.stack([field_real, field_imag], 1)
    return result_field


def solution(mesh):
    in_specs = (
        P(None, "blk"),
        P(None, "blk"),
        P("blk"),
        P("rhs", None, "blk"),
        P("blk", None),
        P("blk"),
        P(None, "blk"),
        P(None, None, "blk"),
    )
    out_specs = P("rhs", None, "blk")
    return jax.shard_map(
        on_device, mesh=mesh, in_specs=in_specs, out_specs=out_specs, check_vma=False
    )
```

profile of v0, /device:TPU:1, one launch (start us, length us, event | category | flops | bytes accessed | tf_op | source)
XLA Modules:
  0.0 703.4 jit_solution(5454243177161245767)
XLA Ops:
  4.9 14.9 %all-to-all-start = ((s32[128,1,8]{2,1,0:T(1,128)}), s32[128,1,8]{2,1,0:T(1,128)S(1)}, u32[]{:S(2)}, u32[]{:S(2)}) async-start(s32[128,1,8]{2,1,0:T(1,128)} %bitcast.14), calls=%async_computation | async-start | bytes 131072 | tf_op jit(solution)/shard_map/all_to_all | solution.py:121
  22.8 160.4 %all_gather.7 = f32[7,32768]{1,0:T(8,128)S(1)} all-gather(f32[7,256]{1,0:T(8,128)S(1)} %concatenate.3), channel_id=1, replica_groups=mesh['blk'=128,'rhs'=2] {'blk'}, dimensions={1}, use_global_device_ids=true | all-gather | bytes 924672 | tf_op jit(solution)/shard_map/all_gather | solution.py:104
  183.2 151.7 %all-gather = f32[1,2,32768]{2,1,0:T(2,128)S(1)} all-gather(f32[1,2,256]{2,1,0:T(2,128)S(1)} %copy-done.2), channel_id=2, replica_groups=mesh['blk'=128,'rhs'=2] {'blk'}, dimensions={2}, use_global_device_ids=true | all-gather | bytes 264192 | tf_op jit(solution)/shard_map/all_gather | solution.py:105
  334.9 313.9 %while.13 = (s32[]{:T(128)}, f32[1,256]{1,0:T(1,128)S(1)}, f32[1,256]{1,0:T(1,128)S(1)}, f32[64,1,2,512]{3,2,1,0:T(2,128)S(1)}, f32[64,7,512]{2,1,0:T(8,128)S(1)...) while((s32[]{:T(128)}, f32[1,256]{1,0:T(1,128)S(1)}, f32[1,256]{1,0:T(1,128)S(1)}, ...), condition=%wide.region_3.4_spmd.clone, body=%wide.region_0.3_spmd.clone.sunk | while | flops 10487301 | bytes 5321883 | solution.py:73
  335.3 2.4 subtract_multiply_fusion.4
  340.2 2.4 subtract_multiply_fusion.4
  345.1 2.4 subtract_multiply_fusion.4
  350.0 2.4 subtract_multiply_fusion.4
  354.9 2.4 subtract_multiply_fusion.4
  359.8 2.4 subtract_multiply_fusion.4
  364.7 2.4 subtract_multiply_fusion.4
  369.6 2.4 subtract_multiply_fusion.4
  374.5 2.4 subtract_multiply_fusion.4
  384.4 2.4 subtract_multiply_fusion.4
  389.3 2.4 subtract_multiply_fusion.4
  394.2 2.4 subtract_multiply_fusion.4
  399.1 2.4 subtract_multiply_fusion.4
  404.0 2.4 subtract_multiply_fusion.4
  408.9 2.4 subtract_multiply_fusion.4
  649.2 2.8 gather_fusion
  653.4 5.3 all-to-all-start.1
  658.8 11.9 %all-to-all-done.1 = f32[1,2,128,8]{3,1,0,2:T(2,128)S(1)} async-done(((f32[1,2,128,8]{3,1,0,2:T(2,128)}), f32[1,2,128,8]{3,1,0,2:T(2,128)S(1)}, u32[]{:S(2)}, u32[]{:S(2)}) %all-to-all-start.1) | async-done | bytes 8224 | tf_op jit(solution)/shard_map/all_to_all | solution.py:123
  672.2 27.7 %gather_fusion.2 = f32[8192,2]{1,0:T(8,128)} fusion(f32[2,256]{0,1:T(8,128)S(1)} %bitcast.135, s32[8192]{0:T(1024)S(1)} %broadcast_clamp_fusion), kind=kCustom, calls=%fused_computation.2 | custom fusion | bytes 163840 | tf_op jit(solution)/shard_map/gather | solution.py:78
  699.9 2.9 copy.29
  (791 shorter events, 286.1 us)
Async XLA Ops:
  0.0 334.9 %copy-start = (f32[3,256]{1,0:T(4,128)S(1)}, f32[3,256]{1,0:T(4,128)}, u32[]{:S(2)}) copy-start(f32[3,256]{1,0:T(4,128)} %param.10) | copy-start | bytes 9220
  0.0 183.2 %copy-start.2 = (f32[1,2,256]{2,1,0:T(2,128)S(1)}, f32[1,2,256]{2,1,0:T(2,128)}, u32[]{:S(2)}) copy-start(f32[1,2,256]{2,1,0:T(2,128)} %param.13) | copy-start | bytes 6148
  4.9 644.1 %all-to-all-start = ((s32[128,1,8]{2,1,0:T(1,128)}), s32[128,1,8]{2,1,0:T(1,128)S(1)}, u32[]{:S(2)}, u32[]{:S(2)}) async-start(s32[128,1,8]{2,1,0:T(1,128)} %bitcast.14), calls=%async_computation | async-start | bytes 131072 | tf_op jit(solution)/shard_map/all_to_all | solution.py:121
  653.4 17.2 %all-to-all-start.1 = ((f32[1,2,128,8]{3,1,0,2:T(2,128)}), f32[1,2,128,8]{3,1,0,2:T(2,128)S(1)}, u32[]{:S(2)}, u32[]{:S(2)}) async-start(f32[1,2,128,8]{3,1,0,2:T(2,128)} %bitcast.18), calls=%async_computation.1 | async-start | bytes 262144 | tf_op jit(solution)/shard_map/all_to_all | solution.py:123
  699.9 2.9 copy-start.1
where the time goes:
time: 704 us; the launch traced here: 703 us
  blocking collectives  312 us (44%)
  other arithmetic  179 us (25%)
  matrix products  133 us (19%)
  local copies, waits for them, and re-layouts  42.6 us (6%)
  starting transfers between devices  20.2 us (3%)
  waiting for transfers between devices  11.9 us (2%)
    all_gather x1, blocking collectives, on_device(): lax.all_gather(geometry, 'blk', axis=1, tiled=True)  160 us
    mul x64, other arithmetic, kernel_tile(): weight * (double * (sines - phases * cosine) - COUPLE * single * cosine)  152 us
    all_gather x1, blocking collectives, on_device(): lax.all_gather(send_density, 'blk', axis=1, tiled=True)  152 us
    dot_general x64, matrix products, apply_tile(): jnp.einsum('ts,rs->rt', imag_part, src_imag, precision=highest)  33.7 us
    dot_general x64, matrix products, apply_tile(): jnp.einsum('ts,rs->rt', imag_part, src_real, precision=highest)  33.6 us
    dot_general x64, matrix products, apply_tile(): jnp.einsum('ts,rs->rt', real_part, src_real, precision=highest)  33.6 us
    dot_general x64, matrix products, apply_tile(): jnp.einsum('ts,rs->rt', real_part, src_imag, precision=highest)  32.5 us
    gather x2, local copies, waits for them, and re-layouts, near_field(): looked = needed[:, :, near_rows]  30.6 us
  transfers between devices with their start and end apart: 2, of which 1 were waited for; matrix products, arithmetic and copies ran while one was open for 45% of the time, Pallas kernels for 0%

commit v1 on v0

v1 whole, which is shorter than its diff:
```python
import functools
import math

import jax
import jax.numpy as jnp
from jax import lax
from jax.experimental import pallas as pl
from jax.experimental.pallas import tpu as pltpu
from jax.sharding import PartitionSpec as P

F32 = jnp.float32
BF16 = jnp.bfloat16
MESH = pl.DeviceIdType.MESH

WAVE = 8.0
SOFT = 0.1
TWO_PI = 2.0 * math.pi
TURNS = WAVE / TWO_PI
TURNS2 = TURNS * TURNS
KAPPA = 1.0 / TWO_PI
MAGIC = 12582912.0

C0 = 2.221441438377396
C1 = -0.9135295479465378
C2 = 0.11267874257383814
C3 = -0.006494477491585805

NY, NZ, NX, NC = 4, 8, 2, 2
PAIRS = NY * NZ
CHUNK = 16


def half_circle(turns):
    v = turns - ((turns + MAGIC) - MAGIC)
    z = v * v
    s = v * (C0 + z * (C1 + z * (C2 + z * C3)))
    q = s * s
    w = 2.0 - q
    s2 = s * (w * lax.rsqrt(w))
    return 0.5 - s2 * s2, s2 * (1.0 - q)


def pair_kernel(turns2, facing):
    h = lax.rsqrt(turns2)
    cosine, sine = half_circle(turns2 * h)
    p = facing * (h * h)
    hk = h * KAPPA
    a = p * hk
    e = p + hk
    return a * cosine + e * sine, a * sine - e * cosine


def split3(x):
    hi = x.astype(BF16).astype(F32)
    rest = x - hi
    mid = rest.astype(BF16).astype(F32)
    return hi, mid, rest - mid


def split2(x):
    hi = x.astype(BF16)
    return hi, (x - hi.astype(F32)).astype(BF16)


def source_terms(geo):
    parts = split3(geo)
    count = geo.shape[1]
    row = lax.broadcasted_iota(jnp.int32, (4, count), 0)

    def stack(k):
        hi, mid, lo = (part[4 * k : 4 * k + 4] for part in parts)
        ones = jnp.where(row < 3, 1.0 if k == 0 else 0.0, 0.0)
        rows = [hi, mid, lo, hi, mid, hi, ones, jnp.zeros((4, count), F32)]
        return jnp.concatenate(rows, 0).astype(BF16)

    return jnp.concatenate([stack(0), stack(1)], 1)


def target_terms(pos):
    count = pos.shape[1]
    hi, mid, lo = split3(pos)
    square = split3(TURNS2 * jnp.sum(pos * pos, 0, keepdims=True))
    one = jnp.ones((1, count), F32)
    zero = jnp.zeros((1, count), F32)
    rows = [hi, one, hi, one, hi, one, mid, zero, mid, zero, lo, zero]
    rows += [square[0], square[1], square[2]] + [zero] * 5
    return jnp.concatenate(rows, 0).T.astype(BF16)


def alternating(i, n):
    odd = i % 2
    return odd * ((i + 1) // 2) + (1 - odd) * ((n - i // 2) % n)


def kernel(
    pos_ref, ang_ref, area_ref, den_ref, owner_ref, slot_ref, index_ref, coef_ref, out_ref,
    pkt, mine, other, tf, rf0, rf1, k0, k1, acc, part, got,
    swap_send, swap_recv, core_send, core_recv, x_send, x_recv, z_send, y_send, recv, end_send, end_recv,
):
    count = pos_ref.shape[1]
    blk = lax.axis_index("blk")
    rhs = lax.axis_index("rhs")
    core = blk % NC
    x = (blk // NC) % NX
    z = (blk // (NC * NX)) % NZ
    y = blk // (NC * NX * NZ)

    def at(yy, zz, xx, cc):
        return ((yy * NZ + zz) * NX + xx) * NC + cc

    core_peer = at(y, z, x, 1 - core)
    x_peer = at(y, z, 1 - x, core)

    barrier = pltpu.get_barrier_semaphore()
    pl.semaphore_signal(barrier, inc=1, device_id={"rhs": 1 - rhs}, device_id_type=MESH)
    for peer in (core_peer, x_peer):
        pl.semaphore_signal(barrier, inc=1, device_id={"blk": peer}, device_id_type=MESH)
    for step in range(1, NZ):
        peer = at(y, (z + step) % NZ, x, core)
        pl.semaphore_signal(barrier, inc=1, device_id={"blk": peer}, device_id_type=MESH)
    for step in range(1, NY):
        peer = at((y + step) % NY, z, x, core)
        pl.semaphore_signal(barrier, inc=1, device_id={"blk": peer}, device_id_type=MESH)

    pos = pos_ref[...]
    cosines, sines = half_circle(ang_ref[...] * KAPPA)
    cosines = 2.0 * cosines
    sines = 2.0 * sines
    normal = jnp.concatenate(
        [cosines[0:1] * cosines[1:2], sines[0:1] * cosines[1:2], sines[1:2]], 0
    )
    weight = area_ref[...] * (TURNS / math.sqrt(count * NY * NZ * NX * NC))
    density = den_ref[0]
    mine[...] = jnp.concatenate([density * weight, density], 0)
    geometry = jnp.concatenate(
        [
            (-2.0 * TURNS2) * pos,
            TURNS2 * (jnp.sum(pos * pos, 0, keepdims=True) + SOFT * SOFT),
            TURNS2 * normal,
            -TURNS2 * jnp.sum(pos * normal, 0, keepdims=True),
        ],
        0,
    )
    tf[...] = target_terms(pos)
    acc[...] = jnp.zeros_like(acc)
    k1[...] = jnp.zeros_like(k1)

    pl.semaphore_wait(barrier, 3 + (NZ - 1) + (NY - 1))

    is_owner = core == rhs

    def swap():
        return pltpu.make_async_remote_copy(
            src_ref=mine, dst_ref=other, send_sem=swap_send, recv_sem=swap_recv,
            device_id={"rhs": 1 - rhs}, device_id_type=MESH,
        )

    def core_copy():
        return pltpu.make_async_remote_copy(
            src_ref=pkt.at[0], dst_ref=pkt.at[0], send_sem=core_send, recv_sem=core_recv,
            device_id={"blk": core_peer}, device_id_type=MESH,
        )

    @pl.when(is_owner)
    def _():
        swap().wait_recv()
        a = mine[...]
        b = other[...]
        first = jnp.where(rhs == 0, a, b)
        second = jnp.where(rhs == 0, b, a)
        pkt[0, 0:8, :] = geometry
        pkt[0, 8:16, :] = jnp.concatenate(
            [first[0:1], second[0:1], first[1:2], second[1:2], first[2:3], second[2:3], first[3:4], second[3:4]], 0
        )
        core_copy().start()

    @pl.when(jnp.logical_not(is_owner))
    def _():
        swap().start()
        core_copy().wait_recv()

    x_copy = pltpu.make_async_remote_copy(
        src_ref=pkt.at[0], dst_ref=pkt.at[1], send_sem=x_send, recv_sem=x_recv,
        device_id={"blk": x_peer}, device_id_type=MESH,
    )
    x_copy.start()
    x_copy.wait_recv()

    def z_copy(i):
        peer = at(y, (z + NZ - alternating(i, NZ)) % NZ, x, core)
        return pltpu.make_async_remote_copy(
            src_ref=pkt.at[pl.ds(0, 2)], dst_ref=pkt.at[pl.ds(2 * i, 2)],
            send_sem=z_send.at[i], recv_sem=recv.at[i],
            device_id={"blk": peer}, device_id_type=MESH,
        )

    def y_copy(i, j):
        peer = at((y + NY - alternating(j, NY)) % NY, z, x, core)
        return pltpu.make_async_remote_copy(
            src_ref=pkt.at[pl.ds(2 * i, 2)], dst_ref=pkt.at[pl.ds(2 * (j * NZ + i), 2)],
            send_sem=y_send.at[j * NZ + i], recv_sem=recv.at[j * NZ + i],
            device_id={"blk": peer}, device_id_type=MESH,
        )

    for i in range(1, NZ):
        z_copy(i).start()
    for j in range(1, NY):
        y_copy(0, j).start()

    rf = (rf0, rf1)
    kk = (k0, k1)

    def products(p, b):
        rf[b][...] = jnp.dot(tf[...], source_terms(pkt[p, 0:8, :]), preferred_element_type=F32)

    def pairs(b):
        for c in range(count // CHUNK):
            rows = slice(c * CHUNK, (c + 1) * CHUNK)
            real, imag = pair_kernel(rf[b][rows, 0:count], rf[b][rows, count : 2 * count])
            real_hi, real_lo = split2(real)
            imag_hi, imag_lo = split2(imag)
            kk[b][rows, 0:count] = real_hi
            kk[b][rows, count : 2 * count] = real_lo
            kk[b][rows, 2 * count : 3 * count] = imag_hi
            kk[b][rows, 3 * count : 4 * count] = imag_lo

    def apply(p, b):
        terms = pkt[p, 8:12, :]
        turned = jnp.concatenate([-terms[2:4], terms[0:2]], 0)

        def both(v):
            hi = v.astype(BF16).astype(F32)
            return jnp.concatenate([hi, v - hi], 0).astype(BF16)

        real, imag = both(terms), both(turned)
        left = jnp.concatenate([real, real, imag, imag], 1)
        acc[...] += lax.dot_general(
            left, kk[b][...], (((1,), (1,)), ((), ())), preferred_element_type=F32
        )

    products(0, 0)

    def body(i, carry):
        p = 2 * i
        apply(jnp.maximum(p - 1, 0), 1)
        products(p + 1, 1)
        pairs(0)

        @pl.when(i + 1 < PAIRS)
        def _():
            pltpu.make_async_remote_copy(
                src_ref=pkt.at[pl.ds(0, 2)], dst_ref=pkt.at[pl.ds(2 * (i + 1), 2)],
                send_sem=x_send, recv_sem=recv.at[i + 1],
                device_id={"blk": x_peer}, device_id_type=MESH,
            ).wait_recv()

        @pl.when(i + 1 < NZ)
        def _():
            for j in range(1, NY):
                y_copy(i + 1, j).start()

        apply(p, 0)
        products(jnp.minimum(p + 2, 2 * PAIRS - 1), 0)
        pairs(1)
        return carry

    lax.fori_loop(0, PAIRS, body, 0)
    apply(2 * PAIRS - 1, 1)
    total = acc[...]
    far = total[0:4] + total[4:8]

    lanes = 128
    halves = count // lanes
    owner = owner_ref[...]
    slot = slot_ref[...]
    listed = [[jnp.zeros((8, lanes), F32) for _ in range(halves)] for _ in range(4)]
    sub = lax.broadcasted_iota(jnp.int32, (8, lanes), 0)
    for group in range(2 * PAIRS // 8):
        k = sub + 8 * group
        pair_i = k // 2
        dz = alternating(pair_i % NZ, NZ)
        dy = alternating(pair_i // NZ, NY)
        block = at((y + dy) % NY, (z + dz) % NZ, (x + k % 2) % NX, rhs)
        for h in range(halves):
            own = jnp.broadcast_to(owner[:, h * lanes : (h + 1) * lanes], (8, lanes))
            place = jnp.broadcast_to(slot[:, h * lanes : (h + 1) * lanes], (8, lanes))
            for t in range(halves):
                hit = jnp.logical_and(own == block, place // lanes == t)
                for c in range(4):
                    table = pkt[8 * group : 8 * group + 8, 12 + c, t * lanes : (t + 1) * lanes]
                    found = jnp.take_along_axis(table, place % lanes, axis=1)
                    listed[c][h] = listed[c][h] + jnp.where(hit, found, 0.0)
    listed = [[jnp.sum(v, 0, keepdims=True) for v in row] for row in listed]

    near = [[], [], [], []]
    neighbours = index_ref.shape[0]
    for h in range(halves):
        sums = [jnp.zeros((8, lanes), F32) for _ in range(4)]
        for m in range(neighbours // 8):
            rows = slice(8 * m, 8 * m + 8)
            cols = slice(h * lanes, (h + 1) * lanes)
            where_to = index_ref[rows, cols]
            looked = []
            for c in range(4):
                value = jnp.zeros((8, lanes), F32)
                for t in range(halves):
                    table = jnp.broadcast_to(listed[c][t], (8, lanes))
                    found = jnp.take_along_axis(table, where_to % lanes, axis=1)
                    value = jnp.where(where_to // lanes == t, found, value)
                looked.append(value)
            real, imag = coef_ref[0, rows, cols], coef_ref[1, rows, cols]
            for r in range(2):
                sums[r] = sums[r] + (real * looked[r] - imag * looked[2 + r])
                sums[2 + r] = sums[2 + r] + (real * looked[2 + r] + imag * looked[r])
        for c in range(4):
            near[c].append(jnp.sum(sums[c], 0, keepdims=True))
    near = jnp.concatenate([jnp.concatenate(row, 1) for row in near], 0)
    both_sides = far + near
    side0 = jnp.concatenate([both_sides[0:1], both_sides[2:3]], 0)
    side1 = jnp.concatenate([both_sides[1:2], both_sides[3:4]], 0)
    part[...] = jnp.where(rhs == 0, side1, side0)
    last = pltpu.make_async_remote_copy(
        src_ref=part, dst_ref=got, send_sem=end_send, recv_sem=end_recv,
        device_id={"rhs": 1 - rhs}, device_id_type=MESH,
    )
    last.start()

    @pl.when(is_owner)
    def _():
        core_copy().wait_send()

    @pl.when(jnp.logical_not(is_owner))
    def _():
        swap().wait_send()

    x_copy.wait_send()
    for i in range(1, NZ):
        z_copy(i).wait_send()

    def drain(i, carry):
        for j in range(1, NY):
            y_copy(i, j).wait_send()
        return carry

    lax.fori_loop(0, NZ, drain, 0)
    last.wait()
    out_ref[0] = 0.5 * density + jnp.where(rhs == 0, side0, side1) + got[...]


def on_device(
    positions, normal_angles, areas, densities, need_owner, need_slot, near_index, near_coef
):
    count = positions.shape[1]
    vmem = pl.BlockSpec(memory_space=pltpu.VMEM)
    dma = pltpu.SemaphoreType.DMA
    return pl.pallas_call(
        kernel,
        out_shape=jax.ShapeDtypeStruct((1, 2, count), F32),
        in_specs=[vmem] * 8,
        out_specs=vmem,
        scratch_shapes=[
            pltpu.VMEM((2 * PAIRS, 16, count), F32),
            pltpu.VMEM((4, count), F32),
            pltpu.VMEM((4, count), F32),
            pltpu.VMEM((count, 32), BF16),
            pltpu.VMEM((count, 2 * count), F32),
            pltpu.VMEM((count, 2 * count), F32),
            pltpu.VMEM((count, 4 * count), BF16),
            pltpu.VMEM((count, 4 * count), BF16),
            pltpu.VMEM((8, count), F32),
            pltpu.VMEM((2, count), F32),
            pltpu.VMEM((2, count), F32),
            dma, dma, dma, dma, dma, dma, dma((NZ,)), dma((PAIRS,)), dma((PAIRS,)), dma, dma,
        ],
        compiler_params=pltpu.CompilerParams(collective_id=0, has_side_effects=True),
        name="field",
    )(
        positions,
        normal_angles,
        areas.reshape(1, count),
        densities,
        need_owner.reshape(1, count),
        need_slot.reshape(1, count),
        near_index,
        near_coef,
    )


def solution(mesh):
    in_specs = (
        P(None, "blk"),
        P(None, "blk"),
        P("blk"),
        P("rhs", None, "blk"),
        P("blk", None),
        P("blk"),
        P(None, "blk"),
        P(None, None, "blk"),
    )
    return jax.shard_map(
        on_device, mesh=mesh, in_specs=in_specs, out_specs=P("rhs", None, "blk"), check_vma=False
    )
```

time: 704 us -> 64.8 us (0.09)
  the two profiles are of different devices: /device:TPU:1 before, /device:TPU:6 now
where the time goes in v1:
time: 64.8 us; the launch traced here: 64.7 us
  Pallas kernels  63.4 us (98%)
  local copies, waits for them, and re-layouts  1.26 us (2%)
    pallas_call x1, Pallas kernels, on_device(): pl.pallas_call(kernel, out_shape=jax.ShapeDtypeStruct((1, 2, count), F32)...  63.4 us

profile of v1, /device:TPU:6, one launch (start us, length us, event | category | flops | bytes accessed | tf_op | source)
XLA Modules:
  0.0 64.7 jit_solution(14225794468136325603)
XLA Ops:
  0.0 63.4 %field.1 = f32[1,2,256]{2,1,0:T(2,128)} custom-call(f32[3,256]{1,0:T(4,128)} %pos_ref.1, f32[2,256]{1,0:T(2,128)} %ang_ref.1, f32[1,256]{1,0:T(1,128)} %bitcast.3, f32[1,2,256]{2,1,0:T(2,128)} %den_ref.1, s32[1,256]{1,0:T(1,128)} %bitcast.4, s32[1,256]{1,0:T(1,128)} %bitcast.5, s32[32,256]{1,0:T(8,128)} %index_ref.1, f32[2,32,256]{2,1,0:T(8,128)} %coef_ref.1), custom_call_target="tpu_custom_call" | custom-call | tf_op jit(solution)/shard_map/field/pallas_call | solution.py:356
  63.4 1.3 %copy.10 = f32[1,2,256]{2,1,0:T(2,128)} copy(f32[1,2,256]{2,1,0:T(2,128)} %field.1) | data formatting | bytes 4096

commit v2 on v1

v2 whole, which is shorter than its diff:
```python
import math

import jax
import jax.numpy as jnp
from jax import lax
from jax.experimental import pallas as pl
from jax.experimental.pallas import tpu as pltpu
from jax.sharding import PartitionSpec as P

F32 = jnp.float32
BF16 = jnp.bfloat16
MESH = pl.DeviceIdType.MESH

WAVE = 8.0
SOFT = 0.1
TWO_PI = 2.0 * math.pi
TURNS = WAVE / TWO_PI
TURNS2 = TURNS * TURNS
KAPPA = 1.0 / TWO_PI
MAGIC = 12582912.0

C0 = 2.221441438377396
C1 = -0.9135295479465378
C2 = 0.11267874257383814
C3 = -0.006494477491585805

NY, NZ, NQ = 4, 8, 4
SIDES = 2
SLOTS = NY * NZ // SIDES
CHUNK = 16
LIST_AT = 12
LANES = 128


def half_circle(turns):
    v = turns - ((turns + MAGIC) - MAGIC)
    z = v * v
    s = v * (C0 + z * (C1 + z * (C2 + z * C3)))
    q = s * s
    w = 2.0 - q
    s2 = s * (w * lax.rsqrt(w))
    return 0.5 - s2 * s2, s2 * (1.0 - q)


def pair_kernel(turns2, facing):
    h = lax.rsqrt(turns2)
    cosine, sine = half_circle(turns2 * h)
    p = facing * (h * h)
    hk = h * KAPPA
    a = p * hk
    e = p + hk
    return a * cosine + e * sine, a * sine - e * cosine


def split3(x):
    hi = x.astype(BF16).astype(F32)
    rest = x - hi
    mid = rest.astype(BF16).astype(F32)
    return hi, mid, rest - mid


def split2(x):
    hi = x.astype(BF16)
    return hi, (x - hi.astype(F32)).astype(BF16)


def source_terms(geo):
    parts = split3(geo)
    count = geo.shape[1]
    row = lax.broadcasted_iota(jnp.int32, (4, count), 0)

    def stack(k):
        hi, mid, lo = (part[4 * k : 4 * k + 4] for part in parts)
        ones = jnp.where(row < 3, 1.0 if k == 0 else 0.0, 0.0)
        rows = [hi, mid, lo, hi, mid, hi, ones, jnp.zeros((4, count), F32)]
        return jnp.concatenate(rows, 0).astype(BF16)

    return jnp.concatenate([stack(0), stack(1)], 1)


def target_terms(pos):
    count = pos.shape[1]
    hi, mid, lo = split3(pos)
    square = split3(TURNS2 * jnp.sum(pos * pos, 0, keepdims=True))
    one = jnp.ones((1, count), F32)
    zero = jnp.zeros((1, count), F32)
    rows = [hi, one, hi, one, hi, one, mid, zero, mid, zero, lo, zero]
    rows += [square[0], square[1], square[2]] + [zero] * 5
    return jnp.concatenate(rows, 0).T.astype(BF16)


def alternating(i, n):
    odd = i % 2
    return odd * ((i + 1) // 2) + (1 - odd) * ((n - i // 2) % n)


def z_offset(i, away):
    odd = i % 2
    return (1 - away) * 2 * alternating(i, NZ // 2) + away * ((1 - odd) * (i + 1) + odd * (NZ - i))


def kernel(
    pos_hbm, ang_hbm, area_hbm, den_hbm, owner_hbm, slot_hbm, index_hbm, coef_hbm, out_ref,
    pos_in, ang_in, area_in, den_in, owner_in, slot_in, index_in, coef_in,
    geo, den, mine, other, tpos, lists, tf, terms, left, rf0, rf1, k0, k1, acc,
    listed, listed_got, part, part_got,
    in_sem, swap_send, swap_recv, geo_send, geo_recv, den_send, den_recv,
    tpos_send, tpos_recv, lists_send, lists_recv, listed_send, listed_recv, part_send, part_recv,
):
    count = pos_hbm.shape[1]
    halves = count // LANES
    blk = lax.axis_index("blk")
    rhs = lax.axis_index("rhs")
    q = blk % NQ
    z = (blk // NQ) % NZ
    y = blk // (NQ * NZ)
    away = (z + rhs) % 2
    is_owner = away == 0

    def block(yy, zz, qq):
        return (yy * NZ + zz) * NQ + qq

    def device(b, r):
        return {"blk": b, "rhs": r}

    def column(n):
        other_q = (q + n // 2) % NQ
        other_r = (rhs + n % 2) % 2
        return other_q, other_r

    barrier = pltpu.get_barrier_semaphore()

    def greet_column(n, carry):
        cq, cr = column(n)
        pl.semaphore_signal(
            barrier, inc=1, device_id=device(block(y, z, cq), cr), device_id_type=MESH
        )
        return carry

    def greet_plane(n, carry):
        pl.semaphore_signal(
            barrier,
            inc=1,
            device_id=device(block((y + n // NZ) % NY, (z + n) % NZ, q), rhs),
            device_id_type=MESH,
        )
        return carry

    lax.fori_loop(1, 2 * NQ, greet_column, 0)
    lax.fori_loop(1, NY * NZ, greet_plane, 0)

    loads = [
        pltpu.make_async_copy(src, dst, in_sem.at[n])
        for n, (src, dst) in enumerate(
            [
                (pos_hbm, pos_in), (ang_hbm, ang_in), (area_hbm, area_in), (den_hbm, den_in),
                (owner_hbm, owner_in), (slot_hbm, slot_in), (index_hbm, index_in), (coef_hbm, coef_in),
            ]
        )
    ]
    for load in loads:
        load.start()
    for load in loads[:6]:
        load.wait()

    pos = pos_in[...]
    tpos[q] = pos
    lists[q] = jnp.concatenate([owner_in[...], slot_in[...]], 0)
    cosines, sines = half_circle(ang_in[...] * KAPPA)
    cosines = 2.0 * cosines
    sines = 2.0 * sines
    normal = jnp.concatenate(
        [cosines[0:1] * cosines[1:2], sines[0:1] * cosines[1:2], sines[1:2]], 0
    )
    weight = area_in[...] * (TURNS / math.sqrt(count * NY * NZ * NQ))
    density = den_in[0]
    mine[...] = jnp.concatenate([density * weight, density], 0)

    @pl.when(is_owner)
    def _():
        geo[0] = jnp.concatenate(
            [
                (-2.0 * TURNS2) * pos,
                TURNS2 * (jnp.sum(pos * pos, 0, keepdims=True) + SOFT * SOFT),
                TURNS2 * normal,
                -TURNS2 * jnp.sum(pos * normal, 0, keepdims=True),
            ],
            0,
        )

    acc[...] = jnp.zeros_like(acc)
    k1[...] = jnp.zeros_like(k1)
    left[...] = jnp.zeros_like(left)

    pl.semaphore_wait(barrier, 2 * NQ - 1 + NY * NZ - 1)

    swap = pltpu.make_async_remote_copy(
        src_ref=mine, dst_ref=other, send_sem=swap_send, recv_sem=swap_recv,
        device_id=device(blk, 1 - rhs), device_id_type=MESH,
    )

    def to_plane(n, src, dst, send, recv):
        slot, far_off = n // 2, n % 2
        zz = (z + NZ - z_offset(slot % NQ, far_off)) % NZ
        yy = (y + NY - alternating(slot // NQ, NY)) % NY
        return pltpu.make_async_remote_copy(
            src_ref=src.at[0], dst_ref=dst.at[slot], send_sem=send.at[n], recv_sem=recv.at[slot],
            device_id=device(block(yy, zz, q), rhs), device_id_type=MESH,
        )

    def geo_copy(n):
        return to_plane(n, geo, geo, geo_send, geo_recv)

    def den_copy(n):
        return to_plane(n, den, den, den_send, den_recv)

    def arrival(dst, recv, slot):
        return pltpu.make_async_remote_copy(
            src_ref=dst.at[0], dst_ref=dst.at[slot], send_sem=swap_send, recv_sem=recv.at[slot],
            device_id=device(blk, 1 - rhs), device_id_type=MESH,
        )

    def to_quarter(n, src, send, recv):
        return pltpu.make_async_remote_copy(
            src_ref=src.at[q], dst_ref=src.at[q], send_sem=send.at[n], recv_sem=recv.at[q],
            device_id=device(block(y, z, (q + n) % NQ), rhs), device_id_type=MESH,
        )

    def from_quarter(n, src, send, recv):
        theirs = (q + n) % NQ
        return pltpu.make_async_remote_copy(
            src_ref=src.at[q], dst_ref=src.at[theirs], send_sem=send.at[n], recv_sem=recv.at[theirs],
            device_id=device(block(y, z, theirs), rhs), device_id_type=MESH,
        )

    def to_column(n, src, dst, send, recv):
        cq, cr = column(n)
        return pltpu.make_async_remote_copy(
            src_ref=src.at[2 * cq + cr], dst_ref=dst.at[2 * q + rhs],
            send_sem=send.at[n], recv_sem=recv.at[2 * q + rhs],
            device_id=device(block(y, z, cq), cr), device_id_type=MESH,
        )

    def from_column(n, src, dst, send, recv):
        cq, cr = column(n)
        return pltpu.make_async_remote_copy(
            src_ref=src.at[2 * cq + cr], dst_ref=dst.at[2 * cq + cr],
            send_sem=send.at[n], recv_sem=recv.at[2 * cq + cr],
            device_id=device(block(y, z, cq), cr), device_id_type=MESH,
        )

    def each(first, last, act):
        def step(n, carry):
            act(n)
            return carry

        lax.fori_loop(first, last, step, 0)

    @pl.when(jnp.logical_not(is_owner))
    def _():
        swap.start()

    each(1, NQ, lambda n: to_quarter(n, tpos, tpos_send, tpos_recv).start())

    @pl.when(is_owner)
    def _():
        each(1, 2 * SLOTS, lambda n: geo_copy(n).start())

    each(1, NQ, lambda n: to_quarter(n, lists, lists_send, lists_recv).start())
    each(1, NQ, lambda n: from_quarter(n, tpos, tpos_send, tpos_recv).wait_recv())
    for j in range(NQ):
        tf[j] = target_terms(tpos[j])

    @pl.when(is_owner)
    def _():
        swap.wait_recv()
        a = mine[...]
        b = other[...]
        first = jnp.where(rhs == 0, a, b)
        second = jnp.where(rhs == 0, b, a)
        den[0] = jnp.concatenate(
            [first[0:1], second[0:1], first[1:2], second[1:2], first[2:3], second[2:3], first[3:4], second[3:4]], 0
        )
        each(1, 2 * SLOTS, lambda n: den_copy(n).start())

    @pl.when(jnp.logical_not(is_owner))
    def _():
        arrival(geo, geo_recv, 0).wait_recv()

    rf = (rf0, rf1)
    kk = (k0, k1)

    def products(j):
        rf[j % 2][...] = jnp.dot(tf[j], terms[...], preferred_element_type=F32)

    def pairs(j):
        b = j % 2
        for c in range(count // CHUNK):
            rows = slice(c * CHUNK, (c + 1) * CHUNK)
            real, imag = pair_kernel(rf[b][rows, 0:count], rf[b][rows, count : 2 * count])
            real_hi, real_lo = split2(real)
            imag_hi, imag_lo = split2(imag)
            kk[b][rows, 0:count] = real_hi
            kk[b][rows, count : 2 * count] = real_lo
            kk[b][rows, 2 * count : 3 * count] = imag_hi
            kk[b][rows, 3 * count : 4 * count] = imag_lo

    def apply(j):
        acc[j] += lax.dot_general(
            left[...], kk[j % 2][...], (((1,), (1,)), ((), ())), preferred_element_type=F32
        )

    def density_terms(p):
        rows = den[p, 0:4, :]
        turned = jnp.concatenate([-rows[2:4], rows[0:2]], 0)

        def both(v):
            hi = v.astype(BF16).astype(F32)
            return jnp.concatenate([hi, v - hi], 0).astype(BF16)

        real, imag = both(rows), both(turned)
        return jnp.concatenate([real, real, imag, imag], 1)

    terms[...] = source_terms(geo[0])
    products(0)

    def look_up():
        each(1, NQ, lambda n: from_quarter(n, lists, lists_send, lists_recv).wait_recv())
        sub = lax.broadcasted_iota(jnp.int32, (8, LANES), 0)
        for j in range(NQ):
            for h in range(halves):
                cols = slice(h * LANES, (h + 1) * LANES)
                own = jnp.broadcast_to(lists[j, 0:1, cols], (8, LANES))
                place = jnp.broadcast_to(lists[j, 1:2, cols], (8, LANES))
                found = [jnp.zeros((8, LANES), F32) for _ in range(4)]
                for group in range(SLOTS // 8):
                    k = sub + 8 * group
                    dz = z_offset(k % NQ, away)
                    dy = alternating(k // NQ, NY)
                    there = block((y + dy) % NY, (z + dz) % NZ, q)
                    for t in range(halves):
                        hit = jnp.logical_and(own == there, place // LANES == t)
                        for c in range(4):
                            table = den[8 * group : 8 * group + 8, 4 + c, t * LANES : (t + 1) * LANES]
                            value = jnp.take_along_axis(table, place % LANES, axis=1)
                            found[c] = found[c] + jnp.where(hit, value, 0.0)
                for c in range(4):
                    listed[2 * j + c % 2, c // 2 : c // 2 + 1, cols] = jnp.sum(found[c], 0, keepdims=True)
        each(1, 2 * NQ, lambda n: to_column(n, listed, listed_got, listed_send, listed_recv).start())

    def body(p, carry):
        @pl.when(jnp.logical_and(p <= LIST_AT, p + away > 0))
        def _():
            arrival(den, den_recv, p).wait_recv()

        @pl.when(p + 1 < SLOTS)
        def _():
            arrival(geo, geo_recv, p + 1).wait_recv()

        @pl.when(p == LIST_AT)
        def _():
            each(LIST_AT + 1, SLOTS, lambda s: arrival(den, den_recv, s).wait_recv())
            look_up()

        apply(3)
        products(1)
        pairs(0)
        left[...] = density_terms(p)
        apply(0)
        products(2)
        pairs(1)
        apply(1)
        products(3)
        pairs(2)
        terms[...] = source_terms(geo[jnp.minimum(p + 1, SLOTS - 1)])
        apply(2)
        products(0)
        pairs(3)
        return carry

    lax.fori_loop(0, SLOTS, body, 0)
    apply(3)
    for j in range(NQ):
        total = acc[j]
        far = total[0:4] + total[4:8]
        for r in range(2):
            part[2 * j + r] = jnp.concatenate([far[r : r + 1], far[2 + r : 3 + r]], 0)
    each(1, 2 * NQ, lambda n: to_column(n, part, part_got, part_send, part_recv).start())

    loads[6].wait()
    loads[7].wait()
    me = 2 * q + rhs
    listed_got[me] = listed[me]
    each(1, 2 * NQ, lambda n: from_column(n, listed, listed_got, listed_send, listed_recv).wait_recv())
    mine_listed = jnp.sum(listed_got[...], 0)
    near = [[], []]
    neighbours = index_hbm.shape[0]
    tables = [
        [
            jnp.broadcast_to(mine_listed[c : c + 1, t * LANES : (t + 1) * LANES], (8, LANES))
            for t in range(halves)
        ]
        for c in range(2)
    ]
    for h in range(halves):
        cols = slice(h * LANES, (h + 1) * LANES)
        sums = [jnp.zeros((8, LANES), F32) for _ in range(2)]
        for m in range(neighbours // 8):
            rows = slice(8 * m, 8 * m + 8)
            where_to = index_in[rows, cols]
            looked = []
            for c in range(2):
                value = jnp.zeros((8, LANES), F32)
                for t in range(halves):
                    found = jnp.take_along_axis(tables[c][t], where_to % LANES, axis=1)
                    value = jnp.where(where_to // LANES == t, found, value)
                looked.append(value)
            real, imag = coef_in[0, rows, cols], coef_in[1, rows, cols]
            sums[0] = sums[0] + (real * looked[0] - imag * looked[1])
            sums[1] = sums[1] + (real * looked[1] + imag * looked[0])
        for c in range(2):
            near[c].append(jnp.sum(sums[c], 0, keepdims=True))
    near = jnp.concatenate([jnp.concatenate(row, 1) for row in near], 0)

    part_got[me] = part[me]

    @pl.when(is_owner)
    def _():
        each(1, 2 * SLOTS, lambda n: geo_copy(n).wait_send())
        each(1, 2 * SLOTS, lambda n: den_copy(n).wait_send())

    @pl.when(jnp.logical_not(is_owner))
    def _():
        swap.wait_send()

    each(1, NQ, lambda n: to_quarter(n, tpos, tpos_send, tpos_recv).wait_send())
    each(1, NQ, lambda n: to_quarter(n, lists, lists_send, lists_recv).wait_send())
    each(1, 2 * NQ, lambda n: to_column(n, listed, listed_got, listed_send, listed_recv).wait_send())
    each(1, 2 * NQ, lambda n: to_column(n, part, part_got, part_send, part_recv).wait_send())
    each(1, 2 * NQ, lambda n: from_column(n, part, part_got, part_send, part_recv).wait_recv())
    out_ref[0] = 0.5 * density + near + jnp.sum(part_got[...], 0)


def on_device(
    positions, normal_angles, areas, densities, need_owner, need_slot, near_index, near_coef
):
    count = positions.shape[1]
    args = (
        positions,
        normal_angles,
        areas.reshape(1, count),
        densities,
        need_owner.reshape(1, count),
        need_slot.reshape(1, count),
        near_index,
        near_coef,
    )
    dma = pltpu.SemaphoreType.DMA
    return pl.pallas_call(
        kernel,
        out_shape=jax.ShapeDtypeStruct((1, 2, count), F32),
        in_specs=[pl.BlockSpec(memory_space=pl.ANY)] * 8,
        out_specs=pl.BlockSpec(memory_space=pltpu.VMEM),
        scratch_shapes=[pltpu.VMEM(arg.shape, arg.dtype) for arg in args]
        + [
            pltpu.VMEM((SLOTS, 8, count), F32),
            pltpu.VMEM((SLOTS, 8, count), F32),
            pltpu.VMEM((4, count), F32),
            pltpu.VMEM((4, count), F32),
            pltpu.VMEM((NQ, 3, count), F32),
            pltpu.VMEM((NQ, 2, count), jnp.int32),
            pltpu.VMEM((NQ, count, 32), BF16),
            pltpu.VMEM((32, 2 * count), BF16),
            pltpu.VMEM((8, 4 * count), BF16),
            pltpu.VMEM((count, 2 * count), F32),
            pltpu.VMEM((count, 2 * count), F32),
            pltpu.VMEM((count, 4 * count), BF16),
            pltpu.VMEM((count, 4 * count), BF16),
            pltpu.VMEM((NQ, 8, count), F32),
            pltpu.VMEM((2 * NQ, 2, count), F32),
            pltpu.VMEM((2 * NQ, 2, count), F32),
            pltpu.VMEM((2 * NQ, 2, count), F32),
            pltpu.VMEM((2 * NQ, 2, count), F32),
            dma((8,)), dma, dma,
            dma((2 * SLOTS,)), dma((SLOTS,)), dma((2 * SLOTS,)), dma((SLOTS,)),
            dma((NQ,)), dma((NQ,)), dma((NQ,)), dma((NQ,)),
            dma((2 * NQ,)), dma((2 * NQ,)), dma((2 * NQ,)), dma((2 * NQ,)),
        ],
        compiler_params=pltpu.CompilerParams(collective_id=0, has_side_effects=True),
        name="field",
    )(*args)


def solution(mesh):
    in_specs = (
        P(None, "blk"),
        P(None, "blk"),
        P("blk"),
        P("rhs", None, "blk"),
        P("blk", None),
        P("blk"),
        P(None, "blk"),
        P(None, None, "blk"),
    )
    return jax.shard_map(
        on_device, mesh=mesh, in_specs=in_specs, out_specs=P("rhs", None, "blk"), check_vma=False
    )
```

time: 64.8 us -> 52.1 us (0.80)
  the two profiles are of different devices: /device:TPU:6 before, /device:TPU:1 now
where the time goes in v2:
time: 52.1 us; the launch traced here: 51.9 us
  Pallas kernels  50.7 us (97%)
  local copies, waits for them, and re-layouts  1.26 us (2%)
    pallas_call x1, Pallas kernels, on_device(): pl.pallas_call(kernel, out_shape=jax.ShapeDtypeStruct((1, 2, count), F32)...  50.7 us
    unnamed x1, local copies, waits for them, and re-layouts  1.26 us

profile of v2, /device:TPU:1, one launch (start us, length us, event | category | flops | bytes accessed | tf_op | source)
XLA Modules:
  0.0 51.9 jit_solution(8400128896554826500)
XLA Ops:
  0.0 50.7 %field.1 = f32[1,2,256]{2,1,0:T(2,128)} custom-call(f32[3,256]{1,0:T(4,128)} %pos_hbm.1, f32[2,256]{1,0:T(2,128)} %ang_hbm.1, f32[1,256]{1,0:T(1,128)} %bitcast.3, f32[1,2,256]{2,1,0:T(2,128)} %den_hbm.1, s32[1,256]{1,0:T(1,128)} %bitcast.4, s32[1,256]{1,0:T(1,128)} %bitcast.5, s32[32,256]{1,0:T(8,128)} %index_hbm.1, f32[2,32,256]{2,1,0:T(8,128)} %coef_hbm.1), custom_call_target="tpu_custom_call" | custom-call | tf_op jit(solution)/shard_map/field/pallas_call | solution.py:459
  50.7 1.3 %copy.10 = f32[1,2,256]{2,1,0:T(2,128)} copy(f32[1,2,256]{2,1,0:T(2,128)} %field.1) | data formatting | bytes 4096

commit v3 on v2

--- a/solution.py
+++ b/solution.py
@@ -17,7 +17,6 @@
 TURNS = WAVE / TWO_PI
 TURNS2 = TURNS * TURNS
 KAPPA = 1.0 / TWO_PI
-MAGIC = 12582912.0
 
 C0 = 2.221441438377396
 C1 = -0.9135295479465378
@@ -33,7 +32,7 @@
 
 
 def half_circle(turns):
-    v = turns - ((turns + MAGIC) - MAGIC)
+    v = turns - jnp.round(turns)
     z = v * v
     s = v * (C0 + z * (C1 + z * (C2 + z * C3)))
     q = s * s
@@ -73,9 +72,9 @@
         hi, mid, lo = (part[4 * k : 4 * k + 4] for part in parts)
         ones = jnp.where(row < 3, 1.0 if k == 0 else 0.0, 0.0)
         rows = [hi, mid, lo, hi, mid, hi, ones, jnp.zeros((4, count), F32)]
-        return jnp.concatenate(rows, 0).astype(BF16)
-
-    return jnp.concatenate([stack(0), stack(1)], 1)
+        return jnp.concatenate(rows, 0).T.astype(BF16)
+
+    return jnp.concatenate([stack(0), stack(1)], 0)
 
 
 def target_terms(pos):
@@ -86,7 +85,7 @@
     zero = jnp.zeros((1, count), F32)
     rows = [hi, one, hi, one, hi, one, mid, zero, mid, zero, lo, zero]
     rows += [square[0], square[1], square[2]] + [zero] * 5
-    return jnp.concatenate(rows, 0).T.astype(BF16)
+    return jnp.concatenate(rows, 0).astype(BF16)
 
 
 def alternating(i, n):
@@ -102,7 +101,7 @@
 def kernel(
     pos_hbm, ang_hbm, area_hbm, den_hbm, owner_hbm, slot_hbm, index_hbm, coef_hbm, out_ref,
     pos_in, ang_in, area_in, den_in, owner_in, slot_in, index_in, coef_in,
-    geo, den, mine, other, tpos, lists, tf, terms, left, rf0, rf1, k0, k1, acc,
+    geo, den, mine, other, tpos, lists, tf, terms, left, rf0, rf1, k0, k1, k2, k3, k4, k5, k6, k7, acc,
     listed, listed_got, part, part_got,
     in_sem, swap_send, swap_recv, geo_send, geo_recv, den_send, den_recv,
     tpos_send, tpos_recv, lists_send, lists_recv, listed_send, listed_recv, part_send, part_recv,
@@ -189,7 +188,8 @@
         )
 
     acc[...] = jnp.zeros_like(acc)
-    k1[...] = jnp.zeros_like(k1)
+    for buffer in (k4, k5, k6, k7):
+        buffer[...] = jnp.zeros_like(buffer)
     left[...] = jnp.zeros_like(left)
 
     pl.semaphore_wait(barrier, 2 * NQ - 1 + NY * NZ - 1)
@@ -288,27 +288,24 @@
         arrival(geo, geo_recv, 0).wait_recv()
 
     rf = (rf0, rf1)
-    kk = (k0, k1)
+    kk = (k0, k1, k2, k3, k4, k5, k6, k7)
 
     def products(j):
-        rf[j % 2][...] = jnp.dot(tf[j], terms[...], preferred_element_type=F32)
-
-    def pairs(j):
-        b = j % 2
+        for half in range(2):
+            rows = slice(half * count, (half + 1) * count)
+            rf[j % 2][rows] = jnp.dot(terms[rows], tf[j % NQ], preferred_element_type=F32)
+
+    def pairs(j, b):
         for c in range(count // CHUNK):
             rows = slice(c * CHUNK, (c + 1) * CHUNK)
-            real, imag = pair_kernel(rf[b][rows, 0:count], rf[b][rows, count : 2 * count])
-            real_hi, real_lo = split2(real)
-            imag_hi, imag_lo = split2(imag)
-            kk[b][rows, 0:count] = real_hi
-            kk[b][rows, count : 2 * count] = real_lo
-            kk[b][rows, 2 * count : 3 * count] = imag_hi
-            kk[b][rows, 3 * count : 4 * count] = imag_lo
-
-    def apply(j):
-        acc[j] += lax.dot_general(
-            left[...], kk[j % 2][...], (((1,), (1,)), ((), ())), preferred_element_type=F32
-        )
+            real, imag = pair_kernel(
+                rf[j % 2][rows], rf[j % 2][count + c * CHUNK : count + (c + 1) * CHUNK]
+            )
+            for n, piece in enumerate(split2(real) + split2(imag)):
+                kk[b][n * count + c * CHUNK : n * count + (c + 1) * CHUNK] = piece
+
+    def apply(j, b):
+        acc[j] += jnp.dot(left[...], kk[b][...], preferred_element_type=F32)
 
     def density_terms(p):
         rows = den[p, 0:4, :]
@@ -348,38 +345,44 @@
                     listed[2 * j + c % 2, c // 2 : c // 2 + 1, cols] = jnp.sum(found[c], 0, keepdims=True)
         each(1, 2 * NQ, lambda n: to_column(n, listed, listed_got, listed_send, listed_recv).start())
 
-    def body(p, carry):
-        @pl.when(jnp.logical_and(p <= LIST_AT, p + away > 0))
+    def packet(p, now):
+        then = 1 - now
+
+        @pl.when(jnp.logical_and(p <= LIST_AT, p + away > 1))
         def _():
-            arrival(den, den_recv, p).wait_recv()
+            arrival(den, den_recv, p - 1).wait_recv()
 
         @pl.when(p + 1 < SLOTS)
         def _():
             arrival(geo, geo_recv, p + 1).wait_recv()
 
-        @pl.when(p == LIST_AT)
+        if now == LIST_AT % 2:
+
+            @pl.when(p == LIST_AT)
+            def _():
+                each(LIST_AT, SLOTS, lambda s: arrival(den, den_recv, s).wait_recv())
+                look_up()
+
+        @pl.when(p > 0)
         def _():
-            each(LIST_AT + 1, SLOTS, lambda s: arrival(den, den_recv, s).wait_recv())
-            look_up()
-
-        apply(3)
-        products(1)
-        pairs(0)
-        left[...] = density_terms(p)
-        apply(0)
-        products(2)
-        pairs(1)
-        apply(1)
-        products(3)
-        pairs(2)
-        terms[...] = source_terms(geo[jnp.minimum(p + 1, SLOTS - 1)])
-        apply(2)
-        products(0)
-        pairs(3)
+            left[...] = density_terms(p - 1)
+
+        for j in range(NQ):
+            apply(j, NQ * then + j)
+            if j == NQ - 1:
+                terms[...] = source_terms(geo[jnp.minimum(p + 1, SLOTS - 1)])
+            products(j + 1)
+            pairs(j, NQ * now + j)
+
+    def body(i, carry):
+        packet(2 * i, 0)
+        packet(2 * i + 1, 1)
         return carry
 
-    lax.fori_loop(0, SLOTS, body, 0)
-    apply(3)
+    lax.fori_loop(0, SLOTS // 2, body, 0)
+    left[...] = density_terms(SLOTS - 1)
+    for j in range(NQ):
+        apply(j, NQ + j)
     for j in range(NQ):
         total = acc[j]
         far = total[0:4] + total[4:8]
@@ -469,13 +472,14 @@
             pltpu.VMEM((4, count), F32),
             pltpu.VMEM((NQ, 3, count), F32),
             pltpu.VMEM((NQ, 2, count), jnp.int32),
-            pltpu.VMEM((NQ, count, 32), BF16),
-            pltpu.VMEM((32, 2 * count), BF16),
+            pltpu.VMEM((NQ, 32, count), BF16),
+            pltpu.VMEM((2 * count, 32), BF16),
             pltpu.VMEM((8, 4 * count), BF16),
-            pltpu.VMEM((count, 2 * count), F32),
-            pltpu.VMEM((count, 2 * count), F32),
-            pltpu.VMEM((count, 4 * count), BF16),
-            pltpu.VMEM((count, 4 * count), BF16),
+            pltpu.VMEM((2 * count, count), F32),
+            pltpu.VMEM((2 * count, count), F32),
+        ]
+        + [pltpu.VMEM((4 * count, count), BF16)] * (2 * NQ)
+        + [
             pltpu.VMEM((NQ, 8, count), F32),
             pltpu.VMEM((2 * NQ, 2, count), F32),
             pltpu.VMEM((2 * NQ, 2, count), F32),

time: 52.1 us -> 50.3 us (0.965)
  Pallas kernels: 50.7 us -> 48.9 us
    pallas_call x1, Pallas kernels: 50.7 us -> 48.9 us  [on_device(): pl.pallas_call(kernel, out_shape=jax.ShapeDtypeStruct((1, 2, count), F32)...]
where the time goes in v3:
time: 50.3 us; the launch traced here: 50.1 us
  Pallas kernels  48.9 us (97%)
  local copies, waits for them, and re-layouts  1.26 us (3%)
    pallas_call x1, Pallas kernels, on_device(): pl.pallas_call(kernel, out_shape=jax.ShapeDtypeStruct((1, 2, count), F32)...  48.9 us
    unnamed x1, local copies, waits for them, and re-layouts  1.26 us

profile of v3, /device:TPU:1, one launch (start us, length us, event | category | flops | bytes accessed | tf_op | source)
XLA Modules:
  0.0 50.1 jit_solution(17557745630877777945)
XLA Ops:
  0.0 48.9 %field.1 = f32[1,2,256]{2,1,0:T(2,128)} custom-call(f32[3,256]{1,0:T(4,128)} %pos_hbm.1, f32[2,256]{1,0:T(2,128)} %ang_hbm.1, f32[1,256]{1,0:T(1,128)} %bitcast.3, f32[1,2,256]{2,1,0:T(2,128)} %den_hbm.1, s32[1,256]{1,0:T(1,128)} %bitcast.4, s32[1,256]{1,0:T(1,128)} %bitcast.5, s32[32,256]{1,0:T(8,128)} %index_hbm.1, f32[2,32,256]{2,1,0:T(8,128)} %coef_hbm.1), custom_call_target="tpu_custom_call" | custom-call | tf_op jit(solution)/shard_map/field/pallas_call | solution.py:462
  48.9 1.3 %copy.10 = f32[1,2,256]{2,1,0:T(2,128)} copy(f32[1,2,256]{2,1,0:T(2,128)} %field.1) | data formatting | bytes 4096

commit v4 on v3

--- a/solution.py
+++ b/solution.py
@@ -24,11 +24,22 @@
 C3 = -0.006494477491585805
 
 NY, NZ, NQ = 4, 8, 4
-SIDES = 2
-SLOTS = NY * NZ // SIDES
+BLOCKS = NY * NZ
+PACKETS = BLOCKS // 2
+EARLY = 8
 CHUNK = 16
 LIST_AT = 12
 LANES = 128
+
+
+def ring(d, n):
+    return min(d, n - d)
+
+
+OFFSETS = sorted(
+    ((dy, dz) for dy in range(NY) for dz in range(NZ)),
+    key=lambda o: (ring(o[0], NY) + ring(o[1], NZ), o),
+)
 
 
 def half_circle(turns):
@@ -88,22 +99,12 @@
     return jnp.concatenate(rows, 0).astype(BF16)
 
 
-def alternating(i, n):
-    odd = i % 2
-    return odd * ((i + 1) // 2) + (1 - odd) * ((n - i // 2) % n)
-
-
-def z_offset(i, away):
-    odd = i % 2
-    return (1 - away) * 2 * alternating(i, NZ // 2) + away * ((1 - odd) * (i + 1) + odd * (NZ - i))
-
-
 def kernel(
     pos_hbm, ang_hbm, area_hbm, den_hbm, owner_hbm, slot_hbm, index_hbm, coef_hbm, out_ref,
     pos_in, ang_in, area_in, den_in, owner_in, slot_in, index_in, coef_in,
-    geo, den, mine, other, tpos, lists, tf, terms, left, rf0, rf1, k0, k1, k2, k3, k4, k5, k6, k7, acc,
+    pkt, mine, other, tpos, lists, tf, terms, left, rf0, rf1, k0, k1, k2, k3, k4, k5, k6, k7, acc,
     listed, listed_got, part, part_got,
-    in_sem, swap_send, swap_recv, geo_send, geo_recv, den_send, den_recv,
+    in_sem, swap_send, swap_recv, pkt_send, pkt_recv, den_send, den_recv,
     tpos_send, tpos_recv, lists_send, lists_recv, listed_send, listed_recv, part_send, part_recv,
 ):
     count = pos_hbm.shape[1]
@@ -113,40 +114,30 @@
     q = blk % NQ
     z = (blk // NQ) % NZ
     y = blk // (NQ * NZ)
-    away = (z + rhs) % 2
-    is_owner = away == 0
-
-    def block(yy, zz, qq):
-        return (yy * NZ + zz) * NQ + qq
+    column_base = blk - q
+    side = 1 - rhs
+    zs = [lax.rem(z + d, NZ) * NQ + q for d in range(NZ)]
+    ys = [lax.rem(y + d, NY) * (NZ * NQ) for d in range(NY)]
+    qs = [lax.rem(q + d, NQ) for d in range(NQ)]
 
     def device(b, r):
         return {"blk": b, "rhs": r}
 
     def column(n):
-        other_q = (q + n // 2) % NQ
-        other_r = (rhs + n % 2) % 2
-        return other_q, other_r
+        return qs[n // 2], (side if n % 2 else rhs)
+
+    def plane(n):
+        dy, dz = OFFSETS[n]
+        return device(ys[(NY - dy) % NY] + zs[(NZ - dz) % NZ], rhs)
 
     barrier = pltpu.get_barrier_semaphore()
-
-    def greet_column(n, carry):
+    for n in range(BLOCKS - 1, 0, -1):
+        pl.semaphore_signal(barrier, inc=1, device_id=plane(n), device_id_type=MESH)
+    for n in range(1, 2 * NQ):
         cq, cr = column(n)
         pl.semaphore_signal(
-            barrier, inc=1, device_id=device(block(y, z, cq), cr), device_id_type=MESH
-        )
-        return carry
-
-    def greet_plane(n, carry):
-        pl.semaphore_signal(
-            barrier,
-            inc=1,
-            device_id=device(block((y + n // NZ) % NY, (z + n) % NZ, q), rhs),
-            device_id_type=MESH,
-        )
-        return carry
-
-    lax.fori_loop(1, 2 * NQ, greet_column, 0)
-    lax.fori_loop(1, NY * NZ, greet_plane, 0)
+            barrier, inc=1, device_id=device(column_base + cq, cr), device_id_type=MESH
+        )
 
     loads = [
         pltpu.make_async_copy(src, dst, in_sem.at[n])
@@ -161,6 +152,12 @@
         load.start()
     for load in loads[:6]:
         load.wait()
+
+    def own_half(v):
+        return jnp.where(rhs == 0, v[:, 0:LANES], v[:, LANES : 2 * LANES])
+
+    def other_half(v):
+        return jnp.where(rhs == 0, v[:, LANES : 2 * LANES], v[:, 0:LANES])
 
     pos = pos_in[...]
     tpos[q] = pos
@@ -171,13 +168,12 @@
     normal = jnp.concatenate(
         [cosines[0:1] * cosines[1:2], sines[0:1] * cosines[1:2], sines[1:2]], 0
     )
-    weight = area_in[...] * (TURNS / math.sqrt(count * NY * NZ * NQ))
+    weight = area_in[...] * (TURNS / math.sqrt(count * BLOCKS * NQ))
     density = den_in[0]
-    mine[...] = jnp.concatenate([density * weight, density], 0)
-
-    @pl.when(is_owner)
-    def _():
-        geo[0] = jnp.concatenate(
+    sources = jnp.concatenate([density * weight, density], 0)
+    mine[...] = other_half(sources)
+    pkt[0, 0:8, 0:LANES] = own_half(
+        jnp.concatenate(
             [
                 (-2.0 * TURNS2) * pos,
                 TURNS2 * (jnp.sum(pos * pos, 0, keepdims=True) + SOFT * SOFT),
@@ -186,51 +182,52 @@
             ],
             0,
         )
-
-    acc[...] = jnp.zeros_like(acc)
-    for buffer in (k4, k5, k6, k7):
-        buffer[...] = jnp.zeros_like(buffer)
-    left[...] = jnp.zeros_like(left)
-
-    pl.semaphore_wait(barrier, 2 * NQ - 1 + NY * NZ - 1)
+    )
+
+    pl.semaphore_wait(barrier, 2 * NQ - 1 + BLOCKS - 1)
 
     swap = pltpu.make_async_remote_copy(
         src_ref=mine, dst_ref=other, send_sem=swap_send, recv_sem=swap_recv,
-        device_id=device(blk, 1 - rhs), device_id_type=MESH,
+        device_id=device(blk, side), device_id_type=MESH,
     )
 
-    def to_plane(n, src, dst, send, recv):
-        slot, far_off = n // 2, n % 2
-        zz = (z + NZ - z_offset(slot % NQ, far_off)) % NZ
-        yy = (y + NY - alternating(slot // NQ, NY)) % NY
-        return pltpu.make_async_remote_copy(
-            src_ref=src.at[0], dst_ref=dst.at[slot], send_sem=send.at[n], recv_sem=recv.at[slot],
-            device_id=device(block(yy, zz, q), rhs), device_id_type=MESH,
-        )
-
-    def geo_copy(n):
-        return to_plane(n, geo, geo, geo_send, geo_recv)
-
-    def den_copy(n):
-        return to_plane(n, den, den, den_send, den_recv)
-
-    def arrival(dst, recv, slot):
-        return pltpu.make_async_remote_copy(
-            src_ref=dst.at[0], dst_ref=dst.at[slot], send_sem=swap_send, recv_sem=recv.at[slot],
-            device_id=device(blk, 1 - rhs), device_id_type=MESH,
+    def lanes_of(n):
+        return pl.ds((n % 2) * LANES, LANES)
+
+    def plane_copy(n, rows, send, recv):
+        return pltpu.make_async_remote_copy(
+            src_ref=pkt.at[0, rows, pl.ds(0, LANES)], dst_ref=pkt.at[n // 2, rows, lanes_of(n)],
+            send_sem=send.at[n], recv_sem=recv.at[n],
+            device_id=plane(n), device_id_type=MESH,
+        )
+
+    geo_rows, den_rows, all_rows = pl.ds(0, 8), pl.ds(8, 8), pl.ds(0, 16)
+
+    def arrival(k, half, rows, recv):
+        return pltpu.make_async_remote_copy(
+            src_ref=pkt.at[0, rows, pl.ds(0, LANES)],
+            dst_ref=pkt.at[k, rows, pl.ds(half * LANES, LANES)],
+            send_sem=swap_send, recv_sem=recv.at[2 * k + half],
+            device_id=device(blk, side), device_id_type=MESH,
+        )
+
+    def sent(n, rows, send):
+        return pltpu.make_async_remote_copy(
+            src_ref=pkt.at[0, rows, pl.ds(0, LANES)], dst_ref=pkt.at[0, rows, pl.ds(0, LANES)],
+            send_sem=send.at[n], recv_sem=swap_recv,
+            device_id=device(blk, side), device_id_type=MESH,
         )
 
     def to_quarter(n, src, send, recv):
         return pltpu.make_async_remote_copy(
             src_ref=src.at[q], dst_ref=src.at[q], send_sem=send.at[n], recv_sem=recv.at[q],
-            device_id=device(block(y, z, (q + n) % NQ), rhs), device_id_type=MESH,
+            device_id=device(column_base + qs[n], rhs), device_id_type=MESH,
         )
 
     def from_quarter(n, src, send, recv):
-        theirs = (q + n) % NQ
-        return pltpu.make_async_remote_copy(
-            src_ref=src.at[q], dst_ref=src.at[theirs], send_sem=send.at[n], recv_sem=recv.at[theirs],
-            device_id=device(block(y, z, theirs), rhs), device_id_type=MESH,
+        return pltpu.make_async_remote_copy(
+            src_ref=src.at[q], dst_ref=src.at[qs[n]], send_sem=send.at[n], recv_sem=recv.at[qs[n]],
+            device_id=device(column_base + qs[n], rhs), device_id_type=MESH,
         )
 
     def to_column(n, src, dst, send, recv):
@@ -238,7 +235,7 @@
         return pltpu.make_async_remote_copy(
             src_ref=src.at[2 * cq + cr], dst_ref=dst.at[2 * q + rhs],
             send_sem=send.at[n], recv_sem=recv.at[2 * q + rhs],
-            device_id=device(block(y, z, cq), cr), device_id_type=MESH,
+            device_id=device(column_base + cq, cr), device_id_type=MESH,
         )
 
     def from_column(n, src, dst, send, recv):
@@ -246,46 +243,41 @@
         return pltpu.make_async_remote_copy(
             src_ref=src.at[2 * cq + cr], dst_ref=dst.at[2 * cq + cr],
             send_sem=send.at[n], recv_sem=recv.at[2 * cq + cr],
-            device_id=device(block(y, z, cq), cr), device_id_type=MESH,
+            device_id=device(column_base + cq, cr), device_id_type=MESH,
         )
 
     def each(first, last, act):
+        for n in range(first, last):
+            act(n)
+
+    def loop(first, last, act):
         def step(n, carry):
             act(n)
             return carry
 
         lax.fori_loop(first, last, step, 0)
 
-    @pl.when(jnp.logical_not(is_owner))
-    def _():
-        swap.start()
-
+    swap.start()
     each(1, NQ, lambda n: to_quarter(n, tpos, tpos_send, tpos_recv).start())
-
-    @pl.when(is_owner)
-    def _():
-        each(1, 2 * SLOTS, lambda n: geo_copy(n).start())
-
+    each(1, EARLY, lambda n: plane_copy(n, geo_rows, pkt_send, pkt_recv).start())
     each(1, NQ, lambda n: to_quarter(n, lists, lists_send, lists_recv).start())
+
+    def send_densities():
+        swap.wait_recv()
+        a = own_half(sources)
+        b = other[...]
+        first = jnp.where(rhs == 0, a, b)
+        second = jnp.where(rhs == 0, b, a)
+        pkt[0, 8:16, 0:LANES] = jnp.concatenate(
+            [first[0:1], second[0:1], first[1:2], second[1:2], first[2:3], second[2:3], first[3:4], second[3:4]], 0
+        )
+        each(1, EARLY, lambda n: plane_copy(n, den_rows, den_send, den_recv).start())
+        each(EARLY, BLOCKS, lambda n: plane_copy(n, all_rows, pkt_send, pkt_recv).start())
+
     each(1, NQ, lambda n: from_quarter(n, tpos, tpos_send, tpos_recv).wait_recv())
     for j in range(NQ):
         tf[j] = target_terms(tpos[j])
-
-    @pl.when(is_owner)
-    def _():
-        swap.wait_recv()
-        a = mine[...]
-        b = other[...]
-        first = jnp.where(rhs == 0, a, b)
-        second = jnp.where(rhs == 0, b, a)
-        den[0] = jnp.concatenate(
-            [first[0:1], second[0:1], first[1:2], second[1:2], first[2:3], second[2:3], first[3:4], second[3:4]], 0
-        )
-        each(1, 2 * SLOTS, lambda n: den_copy(n).start())
-
-    @pl.when(jnp.logical_not(is_owner))
-    def _():
-        arrival(geo, geo_recv, 0).wait_recv()
+    arrival(0, 1, geo_rows, pkt_recv).wait_recv()
 
     rf = (rf0, rf1)
     kk = (k0, k1, k2, k3, k4, k5, k6, k7)
@@ -308,7 +300,7 @@
         acc[j] += jnp.dot(left[...], kk[b][...], preferred_element_type=F32)
 
     def density_terms(p):
-        rows = den[p, 0:4, :]
+        rows = pkt[p, 8:12, :]
         turned = jnp.concatenate([-rows[2:4], rows[0:2]], 0)
 
         def both(v):
@@ -318,27 +310,33 @@
         real, imag = both(rows), both(turned)
         return jnp.concatenate([real, real, imag, imag], 1)
 
-    terms[...] = source_terms(geo[0])
+    terms[...] = source_terms(pkt[0, 0:8, :])
     products(0)
+    send_densities()
 
     def look_up():
         each(1, NQ, lambda n: from_quarter(n, lists, lists_send, lists_recv).wait_recv())
         sub = lax.broadcasted_iota(jnp.int32, (8, LANES), 0)
+        homes = []
+        for group in range(PACKETS // 8):
+            homes.append([])
+            for t in range(halves):
+                home = jnp.zeros((8, LANES), jnp.int32)
+                for row in range(8):
+                    dy, dz = OFFSETS[2 * (8 * group + row) + t]
+                    home = jnp.where(sub == row, ys[dy] + zs[dz], home)
+                homes[group].append(home)
         for j in range(NQ):
             for h in range(halves):
                 cols = slice(h * LANES, (h + 1) * LANES)
                 own = jnp.broadcast_to(lists[j, 0:1, cols], (8, LANES))
                 place = jnp.broadcast_to(lists[j, 1:2, cols], (8, LANES))
                 found = [jnp.zeros((8, LANES), F32) for _ in range(4)]
-                for group in range(SLOTS // 8):
-                    k = sub + 8 * group
-                    dz = z_offset(k % NQ, away)
-                    dy = alternating(k // NQ, NY)
-                    there = block((y + dy) % NY, (z + dz) % NZ, q)
+                for group in range(PACKETS // 8):
                     for t in range(halves):
-                        hit = jnp.logical_and(own == there, place // LANES == t)
+                        hit = jnp.logical_and(own == homes[group][t], place // LANES == rhs)
                         for c in range(4):
-                            table = den[8 * group : 8 * group + 8, 4 + c, t * LANES : (t + 1) * LANES]
+                            table = pkt[8 * group : 8 * group + 8, 12 + c, t * LANES : (t + 1) * LANES]
                             value = jnp.take_along_axis(table, place % LANES, axis=1)
                             found[c] = found[c] + jnp.where(hit, value, 0.0)
                 for c in range(4):
@@ -348,19 +346,33 @@
     def packet(p, now):
         then = 1 - now
 
-        @pl.when(jnp.logical_and(p <= LIST_AT, p + away > 1))
+        @pl.when(jnp.logical_and(p > 1, p <= EARLY // 2))
         def _():
-            arrival(den, den_recv, p - 1).wait_recv()
-
-        @pl.when(p + 1 < SLOTS)
+            for half in range(2):
+                arrival(p - 1, half, den_rows, den_recv).wait_recv()
+
+        @pl.when(p == 1)
         def _():
-            arrival(geo, geo_recv, p + 1).wait_recv()
+            arrival(0, 1, den_rows, den_recv).wait_recv()
+            acc[...] = jnp.zeros_like(acc)
+
+        @pl.when(p + 1 < EARLY // 2)
+        def _():
+            for half in range(2):
+                arrival(p + 1, half, geo_rows, pkt_recv).wait_recv()
+
+        @pl.when(jnp.logical_and(p + 1 >= EARLY // 2, p < LIST_AT))
+        def _():
+            for half in range(2):
+                arrival(p + 1, half, all_rows, pkt_recv).wait_recv()
 
         if now == LIST_AT % 2:
 
             @pl.when(p == LIST_AT)
             def _():
-                each(LIST_AT, SLOTS, lambda s: arrival(den, den_recv, s).wait_recv())
+                for k in range(LIST_AT + 1, PACKETS):
+                    for half in range(2):
+                        arrival(k, half, all_rows, pkt_recv).wait_recv()
                 look_up()
 
         @pl.when(p > 0)
@@ -370,7 +382,7 @@
         for j in range(NQ):
             apply(j, NQ * then + j)
             if j == NQ - 1:
-                terms[...] = source_terms(geo[jnp.minimum(p + 1, SLOTS - 1)])
+                terms[...] = source_terms(pkt[jnp.minimum(p + 1, PACKETS - 1), 0:8, :])
             products(j + 1)
             pairs(j, NQ * now + j)
 
@@ -379,8 +391,8 @@
         packet(2 * i + 1, 1)
         return carry
 
-    lax.fori_loop(0, SLOTS // 2, body, 0)
-    left[...] = density_terms(SLOTS - 1)
+    lax.fori_loop(0, PACKETS // 2, body, 0)
+    left[...] = density_terms(PACKETS - 1)
     for j in range(NQ):
         apply(j, NQ + j)
     for j in range(NQ):
@@ -427,15 +439,10 @@
 
     part_got[me] = part[me]
 
-    @pl.when(is_owner)
-    def _():
-        each(1, 2 * SLOTS, lambda n: geo_copy(n).wait_send())
-        each(1, 2 * SLOTS, lambda n: den_copy(n).wait_send())
-
-    @pl.when(jnp.logical_not(is_owner))
-    def _():
-        swap.wait_send()
-
+    swap.wait_send()
+    loop(1, EARLY, lambda n: sent(n, geo_rows, pkt_send).wait_send())
+    loop(1, EARLY, lambda n: sent(n, den_rows, den_send).wait_send())
+    loop(EARLY, BLOCKS, lambda n: sent(n, all_rows, pkt_send).wait_send())
     each(1, NQ, lambda n: to_quarter(n, tpos, tpos_send, tpos_recv).wait_send())
     each(1, NQ, lambda n: to_quarter(n, lists, lists_send, lists_recv).wait_send())
     each(1, 2 * NQ, lambda n: to_column(n, listed, listed_got, listed_send, listed_recv).wait_send())
@@ -466,10 +473,9 @@
         out_specs=pl.BlockSpec(memory_space=pltpu.VMEM),
         scratch_shapes=[pltpu.VMEM(arg.shape, arg.dtype) for arg in args]
         + [
-            pltpu.VMEM((SLOTS, 8, count), F32),
-            pltpu.VMEM((SLOTS, 8, count), F32),
-            pltpu.VMEM((4, count), F32),
-            pltpu.VMEM((4, count), F32),
+            pltpu.VMEM((PACKETS, 16, count), F32),
+            pltpu.VMEM((4, LANES), F32),
+            pltpu.VMEM((4, LANES), F32),
             pltpu.VMEM((NQ, 3, count), F32),
             pltpu.VMEM((NQ, 2, count), jnp.int32),
             pltpu.VMEM((NQ, 32, count), BF16),
@@ -486,7 +492,7 @@
             pltpu.VMEM((2 * NQ, 2, count), F32),
             pltpu.VMEM((2 * NQ, 2, count), F32),
             dma((8,)), dma, dma,
-            dma((2 * SLOTS,)), dma((SLOTS,)), dma((2 * SLOTS,)), dma((SLOTS,)),
+            dma((BLOCKS,)), dma((BLOCKS,)), dma((EARLY,)), dma((EARLY,)),
             dma((NQ,)), dma((NQ,)), dma((NQ,)), dma((NQ,)),
             dma((2 * NQ,)), dma((2 * NQ,)), dma((2 * NQ,)), dma((2 * NQ,)),
         ],

time: 50.3 us -> 51 us (1.014)
  Pallas kernels: 48.9 us -> 49.6 us
    pallas_call x1, Pallas kernels: 48.9 us -> 49.6 us  [on_device(): pl.pallas_call(kernel, out_shape=jax.ShapeDtypeStruct((1, 2, count), F32)...]
where the time goes in v4:
time: 51 us; the launch traced here: 50.9 us
  Pallas kernels  49.6 us (97%)
  local copies, waits for them, and re-layouts  1.26 us (2%)
    pallas_call x1, Pallas kernels, on_device(): pl.pallas_call(kernel, out_shape=jax.ShapeDtypeStruct((1, 2, count), F32)...  49.6 us
    unnamed x1, local copies, waits for them, and re-layouts  1.26 us

profile of v4, /device:TPU:1, one launch (start us, length us, event | category | flops | bytes accessed | tf_op | source)
XLA Modules:
  0.0 50.9 jit_solution(15830224135204805210)
XLA Ops:
  0.0 49.6 %field.1 = f32[1,2,256]{2,1,0:T(2,128)} custom-call(f32[3,256]{1,0:T(4,128)} %pos_hbm.1, f32[2,256]{1,0:T(2,128)} %ang_hbm.1, f32[1,256]{1,0:T(1,128)} %bitcast.3, f32[1,2,256]{2,1,0:T(2,128)} %den_hbm.1, s32[1,256]{1,0:T(1,128)} %bitcast.4, s32[1,256]{1,0:T(1,128)} %bitcast.5, s32[32,256]{1,0:T(8,128)} %index_hbm.1, f32[2,32,256]{2,1,0:T(8,128)} %coef_hbm.1), custom_call_target="tpu_custom_call" | custom-call | tf_op jit(solution)/shard_map/field/pallas_call | solution.py:469
  49.6 1.3 %copy.10 = f32[1,2,256]{2,1,0:T(2,128)} copy(f32[1,2,256]{2,1,0:T(2,128)} %field.1) | data formatting | bytes 4096

commit v5 on v4

--- a/solution.py
+++ b/solution.py
@@ -40,6 +40,12 @@
     ((dy, dz) for dy in range(NY) for dz in range(NZ)),
     key=lambda o: (ring(o[0], NY) + ring(o[1], NZ), o),
 )
+HOPS = [ring(dy, NY) + ring(dz, NZ) for dy, dz in OFFSETS]
+FARTHEST = max(HOPS)
+
+
+def within(hops):
+    return sum(h <= hops for h in HOPS)
 
 
 def half_circle(turns):
@@ -104,7 +110,7 @@
     pos_in, ang_in, area_in, den_in, owner_in, slot_in, index_in, coef_in,
     pkt, mine, other, tpos, lists, tf, terms, left, rf0, rf1, k0, k1, k2, k3, k4, k5, k6, k7, acc,
     listed, listed_got, part, part_got,
-    in_sem, swap_send, swap_recv, pkt_send, pkt_recv, den_send, den_recv,
+    in_sem, round_sem, swap_send, swap_recv, pkt_send, pkt_recv, den_send, den_recv,
     tpos_send, tpos_recv, lists_send, lists_recv, listed_send, listed_recv, part_send, part_recv,
 ):
     count = pos_hbm.shape[1]
@@ -131,7 +137,8 @@
         return device(ys[(NY - dy) % NY] + zs[(NZ - dz) % NZ], rhs)
 
     barrier = pltpu.get_barrier_semaphore()
-    for n in range(BLOCKS - 1, 0, -1):
+    near = within(1)
+    for n in range(1, near):
         pl.semaphore_signal(barrier, inc=1, device_id=plane(n), device_id_type=MESH)
     for n in range(1, 2 * NQ):
         cq, cr = column(n)
@@ -184,7 +191,7 @@
         )
     )
 
-    pl.semaphore_wait(barrier, 2 * NQ - 1 + BLOCKS - 1)
+    pl.semaphore_wait(barrier, 2 * NQ - 1 + near - 1)
 
     swap = pltpu.make_async_remote_copy(
         src_ref=mine, dst_ref=other, send_sem=swap_send, recv_sem=swap_recv,
@@ -257,9 +264,19 @@
 
         lax.fori_loop(first, last, step, 0)
 
+    def tell(r):
+        for n in range(1, near):
+            pl.semaphore_signal(round_sem.at[r], inc=1, device_id=plane(n), device_id_type=MESH)
+
+    def hear(r):
+        pl.semaphore_wait(round_sem.at[r], near - 1)
+        if r < FARTHEST:
+            tell(r + 1)
+
     swap.start()
+    tell(2)
     each(1, NQ, lambda n: to_quarter(n, tpos, tpos_send, tpos_recv).start())
-    each(1, EARLY, lambda n: plane_copy(n, geo_rows, pkt_send, pkt_recv).start())
+    each(1, near, lambda n: plane_copy(n, geo_rows, pkt_send, pkt_recv).start())
     each(1, NQ, lambda n: to_quarter(n, lists, lists_send, lists_recv).start())
 
     def send_densities():
@@ -272,8 +289,10 @@
             [first[0:1], second[0:1], first[1:2], second[1:2], first[2:3], second[2:3], first[3:4], second[3:4]], 0
         )
         each(1, EARLY, lambda n: plane_copy(n, den_rows, den_send, den_recv).start())
-        each(EARLY, BLOCKS, lambda n: plane_copy(n, all_rows, pkt_send, pkt_recv).start())
-
+        each(EARLY, within(2), lambda n: plane_copy(n, all_rows, pkt_send, pkt_recv).start())
+
+    hear(2)
+    each(near, EARLY, lambda n: plane_copy(n, geo_rows, pkt_send, pkt_recv).start())
     each(1, NQ, lambda n: from_quarter(n, tpos, tpos_send, tpos_recv).wait_recv())
     for j in range(NQ):
         tf[j] = target_terms(tpos[j])
@@ -365,6 +384,18 @@
         def _():
             for half in range(2):
                 arrival(p + 1, half, all_rows, pkt_recv).wait_recv()
+
+        for r in range(3, FARTHEST + 1):
+            if now == (r - 2) % 2:
+
+                @pl.when(p == r - 2)
+                def _():
+                    hear(r)
+                    each(
+                        within(r - 1),
+                        within(r),
+                        lambda n: plane_copy(n, all_rows, pkt_send, pkt_recv).start(),
+                    )
 
         if now == LIST_AT % 2:
 
@@ -491,7 +522,7 @@
             pltpu.VMEM((2 * NQ, 2, count), F32),
             pltpu.VMEM((2 * NQ, 2, count), F32),
             pltpu.VMEM((2 * NQ, 2, count), F32),
-            dma((8,)), dma, dma,
+            dma((8,)), pltpu.SemaphoreType.REGULAR((FARTHEST + 1,)), dma, dma,
             dma((BLOCKS,)), dma((BLOCKS,)), dma((EARLY,)), dma((EARLY,)),
             dma((NQ,)), dma((NQ,)), dma((NQ,)), dma((NQ,)),
             dma((2 * NQ,)), dma((2 * NQ,)), dma((2 * NQ,)), dma((2 * NQ,)),

time: 51 us -> 49.1 us (0.963)
  Pallas kernels: 49.6 us -> 47.7 us
    pallas_call x1, Pallas kernels: 49.6 us -> 47.7 us  [on_device(): pl.pallas_call(kernel, out_shape=jax.ShapeDtypeStruct((1, 2, count), F32)...]
where the time goes in v5:
time: 49.1 us; the launch traced here: 49 us
  Pallas kernels  47.7 us (97%)
  local copies, waits for them, and re-layouts  1.26 us (3%)
    pallas_call x1, Pallas kernels, on_device(): pl.pallas_call(kernel, out_shape=jax.ShapeDtypeStruct((1, 2, count), F32)...  47.7 us
    unnamed x1, local copies, waits for them, and re-layouts  1.26 us

profile of v5, /device:TPU:1, one launch (start us, length us, event | category | flops | bytes accessed | tf_op | source)
XLA Modules:
  0.0 49.0 jit_solution(12789330716403093494)
XLA Ops:
  0.0 47.7 %field.1 = f32[1,2,256]{2,1,0:T(2,128)} custom-call(f32[3,256]{1,0:T(4,128)} %pos_hbm.1, f32[2,256]{1,0:T(2,128)} %ang_hbm.1, f32[1,256]{1,0:T(1,128)} %bitcast.3, f32[1,2,256]{2,1,0:T(2,128)} %den_hbm.1, s32[1,256]{1,0:T(1,128)} %bitcast.4, s32[1,256]{1,0:T(1,128)} %bitcast.5, s32[32,256]{1,0:T(8,128)} %index_hbm.1, f32[2,32,256]{2,1,0:T(8,128)} %coef_hbm.1), custom_call_target="tpu_custom_call" | custom-call | tf_op jit(solution)/shard_map/field/pallas_call | solution.py:500
  47.8 1.3 %copy.10 = f32[1,2,256]{2,1,0:T(2,128)} copy(f32[1,2,256]{2,1,0:T(2,128)} %field.1) | data formatting | bytes 4096

commit v6 on v5

--- a/solution.py
+++ b/solution.py
@@ -28,8 +28,9 @@
 PACKETS = BLOCKS // 2
 EARLY = 8
 CHUNK = 16
-LIST_AT = 12
+LIST_AT = 14
 LANES = 128
+ROUND_AT = {3: 2, 4: 4, 5: 7, 6: 9}
 
 
 def ring(d, n):
@@ -386,9 +387,9 @@
                 arrival(p + 1, half, all_rows, pkt_recv).wait_recv()
 
         for r in range(3, FARTHEST + 1):
-            if now == (r - 2) % 2:
-
-                @pl.when(p == r - 2)
+            if now == ROUND_AT[r] % 2:
+
+                @pl.when(p == ROUND_AT[r])
                 def _():
                     hear(r)
                     each(

time: 49.1 us -> 48.1 us (0.980)
  Pallas kernels: 47.7 us -> 46.7 us
    pallas_call x1, Pallas kernels: 47.7 us -> 46.7 us  [on_device(): pl.pallas_call(kernel, out_shape=jax.ShapeDtypeStruct((1, 2, count), F32)...]
where the time goes in v6:
time: 48.1 us; the launch traced here: 48 us
  Pallas kernels  46.7 us (97%)
  local copies, waits for them, and re-layouts  1.26 us (3%)
    pallas_call x1, Pallas kernels, on_device(): pl.pallas_call(kernel, out_shape=jax.ShapeDtypeStruct((1, 2, count), F32)...  46.7 us
    unnamed x1, local copies, waits for them, and re-layouts  1.26 us

profile of v6, /device:TPU:1, one launch (start us, length us, event | category | flops | bytes accessed | tf_op | source)
XLA Modules:
  0.0 48.0 jit_solution(13915189735764775233)
XLA Ops:
  0.0 46.7 %field.1 = f32[1,2,256]{2,1,0:T(2,128)} custom-call(f32[3,256]{1,0:T(4,128)} %pos_hbm.1, f32[2,256]{1,0:T(2,128)} %ang_hbm.1, f32[1,256]{1,0:T(1,128)} %bitcast.3, f32[1,2,256]{2,1,0:T(2,128)} %den_hbm.1, s32[1,256]{1,0:T(1,128)} %bitcast.4, s32[1,256]{1,0:T(1,128)} %bitcast.5, s32[32,256]{1,0:T(8,128)} %index_hbm.1, f32[2,32,256]{2,1,0:T(8,128)} %coef_hbm.1), custom_call_target="tpu_custom_call" | custom-call | tf_op jit(solution)/shard_map/field/pallas_call | solution.py:501
  46.7 1.3 %copy.10 = f32[1,2,256]{2,1,0:T(2,128)} copy(f32[1,2,256]{2,1,0:T(2,128)} %field.1) | data formatting | bytes 4096

commit v7 on v6

--- a/solution.py
+++ b/solution.py
@@ -180,7 +180,7 @@
     density = den_in[0]
     sources = jnp.concatenate([density * weight, density], 0)
     mine[...] = other_half(sources)
-    pkt[0, 0:8, 0:LANES] = own_half(
+    pkt[1, 0:8, 0:LANES] = own_half(
         jnp.concatenate(
             [
                 (-2.0 * TURNS2) * pos,
@@ -204,7 +204,7 @@
 
     def plane_copy(n, rows, send, recv):
         return pltpu.make_async_remote_copy(
-            src_ref=pkt.at[0, rows, pl.ds(0, LANES)], dst_ref=pkt.at[n // 2, rows, lanes_of(n)],
+            src_ref=pkt.at[1, rows, pl.ds(0, LANES)], dst_ref=pkt.at[n // 2 + 1, rows, lanes_of(n)],
             send_sem=send.at[n], recv_sem=recv.at[n],
             device_id=plane(n), device_id_type=MESH,
         )
@@ -213,15 +213,15 @@
 
     def arrival(k, half, rows, recv):
         return pltpu.make_async_remote_copy(
-            src_ref=pkt.at[0, rows, pl.ds(0, LANES)],
-            dst_ref=pkt.at[k, rows, pl.ds(half * LANES, LANES)],
+            src_ref=pkt.at[1, rows, pl.ds(0, LANES)],
+            dst_ref=pkt.at[k + 1, rows, pl.ds(half * LANES, LANES)],
             send_sem=swap_send, recv_sem=recv.at[2 * k + half],
             device_id=device(blk, side), device_id_type=MESH,
         )
 
     def sent(n, rows, send):
         return pltpu.make_async_remote_copy(
-            src_ref=pkt.at[0, rows, pl.ds(0, LANES)], dst_ref=pkt.at[0, rows, pl.ds(0, LANES)],
+            src_ref=pkt.at[1, rows, pl.ds(0, LANES)], dst_ref=pkt.at[1, rows, pl.ds(0, LANES)],
             send_sem=send.at[n], recv_sem=swap_recv,
             device_id=device(blk, side), device_id_type=MESH,
         )
@@ -286,7 +286,7 @@
         b = other[...]
         first = jnp.where(rhs == 0, a, b)
         second = jnp.where(rhs == 0, b, a)
-        pkt[0, 8:16, 0:LANES] = jnp.concatenate(
+        pkt[1, 8:16, 0:LANES] = jnp.concatenate(
             [first[0:1], second[0:1], first[1:2], second[1:2], first[2:3], second[2:3], first[3:4], second[3:4]], 0
         )
         each(1, EARLY, lambda n: plane_copy(n, den_rows, den_send, den_recv).start())
@@ -320,7 +320,7 @@
         acc[j] += jnp.dot(left[...], kk[b][...], preferred_element_type=F32)
 
     def density_terms(p):
-        rows = pkt[p, 8:12, :]
+        rows = pkt[p + 1, 8:12, :]
         turned = jnp.concatenate([-rows[2:4], rows[0:2]], 0)
 
         def both(v):
@@ -330,7 +330,7 @@
         real, imag = both(rows), both(turned)
         return jnp.concatenate([real, real, imag, imag], 1)
 
-    terms[...] = source_terms(pkt[0, 0:8, :])
+    terms[...] = source_terms(pkt[1, 0:8, :])
     products(0)
     send_densities()
 
@@ -356,7 +356,7 @@
                     for t in range(halves):
                         hit = jnp.logical_and(own == homes[group][t], place // LANES == rhs)
                         for c in range(4):
-                            table = pkt[8 * group : 8 * group + 8, 12 + c, t * LANES : (t + 1) * LANES]
+                            table = pkt[8 * group + 1 : 8 * group + 9, 12 + c, t * LANES : (t + 1) * LANES]
                             value = jnp.take_along_axis(table, place % LANES, axis=1)
                             found[c] = found[c] + jnp.where(hit, value, 0.0)
                 for c in range(4):
@@ -407,14 +407,11 @@
                         arrival(k, half, all_rows, pkt_recv).wait_recv()
                 look_up()
 
-        @pl.when(p > 0)
-        def _():
-            left[...] = density_terms(p - 1)
-
+        left[...] = density_terms(p - 1)
         for j in range(NQ):
             apply(j, NQ * then + j)
             if j == NQ - 1:
-                terms[...] = source_terms(pkt[jnp.minimum(p + 1, PACKETS - 1), 0:8, :])
+                terms[...] = source_terms(pkt[jnp.minimum(p + 2, PACKETS), 0:8, :])
             products(j + 1)
             pairs(j, NQ * now + j)
 
@@ -505,7 +502,7 @@
         out_specs=pl.BlockSpec(memory_space=pltpu.VMEM),
         scratch_shapes=[pltpu.VMEM(arg.shape, arg.dtype) for arg in args]
         + [
-            pltpu.VMEM((PACKETS, 16, count), F32),
+            pltpu.VMEM((PACKETS + 1, 16, count), F32),
             pltpu.VMEM((4, LANES), F32),
             pltpu.VMEM((4, LANES), F32),
             pltpu.VMEM((NQ, 3, count), F32),

time: 48.1 us -> 47.9 us (level)
  no operation moved by 1% of the time
where the time goes in v7:
time: 47.9 us; the launch traced here: 47.8 us
  Pallas kernels  46.5 us (97%)
  local copies, waits for them, and re-layouts  1.26 us (3%)
    pallas_call x1, Pallas kernels, on_device(): pl.pallas_call(kernel, out_shape=jax.ShapeDtypeStruct((1, 2, count), F32)...  46.5 us
    unnamed x1, local copies, waits for them, and re-layouts  1.26 us

profile of v7, /device:TPU:1, one launch (start us, length us, event | category | flops | bytes accessed | tf_op | source)
XLA Modules:
  0.0 47.8 jit_solution(14742661732607625554)
XLA Ops:
  0.0 46.5 %field.1 = f32[1,2,256]{2,1,0:T(2,128)} custom-call(f32[3,256]{1,0:T(4,128)} %pos_hbm.1, f32[2,256]{1,0:T(2,128)} %ang_hbm.1, f32[1,256]{1,0:T(1,128)} %bitcast.3, f32[1,2,256]{2,1,0:T(2,128)} %den_hbm.1, s32[1,256]{1,0:T(1,128)} %bitcast.4, s32[1,256]{1,0:T(1,128)} %bitcast.5, s32[32,256]{1,0:T(8,128)} %index_hbm.1, f32[2,32,256]{2,1,0:T(8,128)} %coef_hbm.1), custom_call_target="tpu_custom_call" | custom-call | tf_op jit(solution)/shard_map/field/pallas_call | solution.py:498
  46.5 1.3 %copy.10 = f32[1,2,256]{2,1,0:T(2,128)} copy(f32[1,2,256]{2,1,0:T(2,128)} %field.1) | data formatting | bytes 4096

commit v8 on v7

--- a/solution.py
+++ b/solution.py
@@ -409,10 +409,10 @@
 
         left[...] = density_terms(p - 1)
         for j in range(NQ):
-            apply(j, NQ * then + j)
             if j == NQ - 1:
                 terms[...] = source_terms(pkt[jnp.minimum(p + 2, PACKETS), 0:8, :])
             products(j + 1)
+            apply(j, NQ * then + j)
             pairs(j, NQ * now + j)
 
     def body(i, carry):

time: 47.9 us -> 47 us (0.981)
  Pallas kernels: 46.5 us -> 45.6 us
    pallas_call x1, Pallas kernels: 46.5 us -> 45.6 us  [on_device(): pl.pallas_call(kernel, out_shape=jax.ShapeDtypeStruct((1, 2, count), F32)...]
where the time goes in v8:
time: 47 us; the launch traced here: 46.8 us
  Pallas kernels  45.6 us (97%)
  local copies, waits for them, and re-layouts  1.26 us (3%)
    pallas_call x1, Pallas kernels, on_device(): pl.pallas_call(kernel, out_shape=jax.ShapeDtypeStruct((1, 2, count), F32)...  45.6 us
    unnamed x1, local copies, waits for them, and re-layouts  1.26 us

profile of v8, /device:TPU:1, one launch (start us, length us, event | category | flops | bytes accessed | tf_op | source)
XLA Modules:
  0.0 46.8 jit_solution(2320671656319450669)
XLA Ops:
  0.0 45.6 %field.1 = f32[1,2,256]{2,1,0:T(2,128)} custom-call(f32[3,256]{1,0:T(4,128)} %pos_hbm.1, f32[2,256]{1,0:T(2,128)} %ang_hbm.1, f32[1,256]{1,0:T(1,128)} %bitcast.3, f32[1,2,256]{2,1,0:T(2,128)} %den_hbm.1, s32[1,256]{1,0:T(1,128)} %bitcast.4, s32[1,256]{1,0:T(1,128)} %bitcast.5, s32[32,256]{1,0:T(8,128)} %index_hbm.1, f32[2,32,256]{2,1,0:T(8,128)} %coef_hbm.1), custom_call_target="tpu_custom_call" | custom-call | tf_op jit(solution)/shard_map/field/pallas_call | solution.py:498
  45.6 1.3 %copy.10 = f32[1,2,256]{2,1,0:T(2,128)} copy(f32[1,2,256]{2,1,0:T(2,128)} %field.1) | data formatting | bytes 4096

commit v9 on v8

--- a/solution.py
+++ b/solution.py
@@ -109,7 +109,7 @@
 def kernel(
     pos_hbm, ang_hbm, area_hbm, den_hbm, owner_hbm, slot_hbm, index_hbm, coef_hbm, out_ref,
     pos_in, ang_in, area_in, den_in, owner_in, slot_in, index_in, coef_in,
-    pkt, mine, other, tpos, lists, tf, terms, left, rf0, rf1, k0, k1, k2, k3, k4, k5, k6, k7, acc,
+    pkt, mine, other, tpos, lists, tf, terms, left, left_last, rf0, rf1, k0, k1, k2, k3, k4, k5, k6, k7, acc,
     listed, listed_got, part, part_got,
     in_sem, round_sem, swap_send, swap_recv, pkt_send, pkt_recv, den_send, den_recv,
     tpos_send, tpos_recv, lists_send, lists_recv, listed_send, listed_recv, part_send, part_recv,
@@ -316,8 +316,8 @@
             for n, piece in enumerate(split2(real) + split2(imag)):
                 kk[b][n * count + c * CHUNK : n * count + (c + 1) * CHUNK] = piece
 
-    def apply(j, b):
-        acc[j] += jnp.dot(left[...], kk[b][...], preferred_element_type=F32)
+    def apply(j, b, lhs=left):
+        acc[j] += jnp.dot(lhs[...], kk[b][...], preferred_element_type=F32)
 
     def density_terms(p):
         rows = pkt[p + 1, 8:12, :]
@@ -420,10 +420,18 @@
         packet(2 * i + 1, 1)
         return carry
 
-    lax.fori_loop(0, PACKETS // 2, body, 0)
-    left[...] = density_terms(PACKETS - 1)
+    lax.fori_loop(0, PACKETS // 2 - 1, body, 0)
+    packet(jnp.int32(PACKETS - 2), 0)
+    left[...] = density_terms(PACKETS - 2)
+    left_last[...] = density_terms(PACKETS - 1)
     for j in range(NQ):
-        apply(j, NQ + j)
+        if j < NQ - 1:
+            products(j + 1)
+        apply(j, j)
+        if j > 0:
+            apply(j - 1, NQ + j - 1, left_last)
+        pairs(j, NQ + j)
+    apply(NQ - 1, 2 * NQ - 1, left_last)
     for j in range(NQ):
         total = acc[j]
         far = total[0:4] + total[4:8]
@@ -510,6 +518,7 @@
             pltpu.VMEM((NQ, 32, count), BF16),
             pltpu.VMEM((2 * count, 32), BF16),
             pltpu.VMEM((8, 4 * count), BF16),
+            pltpu.VMEM((8, 4 * count), BF16),
             pltpu.VMEM((2 * count, count), F32),
             pltpu.VMEM((2 * count, count), F32),
         ]

time: 47 us -> 46.8 us (level)
  no operation moved by 1% of the time
where the time goes in v9:
time: 46.8 us; the launch traced here: 46.6 us
  Pallas kernels  45.4 us (97%)
  local copies, waits for them, and re-layouts  1.26 us (3%)
    pallas_call x1, Pallas kernels, on_device(): pl.pallas_call(kernel, out_shape=jax.ShapeDtypeStruct((1, 2, count), F32)...  45.4 us
    unnamed x1, local copies, waits for them, and re-layouts  1.26 us

profile of v9, /device:TPU:1, one launch (start us, length us, event | category | flops | bytes accessed | tf_op | source)
XLA Modules:
  0.0 46.6 jit_solution(14222214935103051492)
XLA Ops:
  0.0 45.4 %field.1 = f32[1,2,256]{2,1,0:T(2,128)} custom-call(f32[3,256]{1,0:T(4,128)} %pos_hbm.1, f32[2,256]{1,0:T(2,128)} %ang_hbm.1, f32[1,256]{1,0:T(1,128)} %bitcast.3, f32[1,2,256]{2,1,0:T(2,128)} %den_hbm.1, s32[1,256]{1,0:T(1,128)} %bitcast.4, s32[1,256]{1,0:T(1,128)} %bitcast.5, s32[32,256]{1,0:T(8,128)} %index_hbm.1, f32[2,32,256]{2,1,0:T(8,128)} %coef_hbm.1), custom_call_target="tpu_custom_call" | custom-call | tf_op jit(solution)/shard_map/field/pallas_call | solution.py:506
  45.4 1.3 %copy.10 = f32[1,2,256]{2,1,0:T(2,128)} copy(f32[1,2,256]{2,1,0:T(2,128)} %field.1) | data formatting | bytes 4096
